TPU v7x, 256 devices: a whole 4x4x8 slice. The times are simulated.
256 devices in a mesh: layer: 64 (over x, z, core), dp: 4 (over y).
Axes of the slice: x: 4, y: 4, z: 8, core: 2. Of those that a mesh axis runs over, the one named last changes fastest.
Arguments:
- cpoints: float32 [64, 4, 64, 1024], P('layer', 'dp'), parts along dimension 1, may hold values from -6 to 6
- network_input: float32 [4, 64, 1024], P('dp'), parts along dimension 0, may hold values from -6 to 6
- conv_weight: bfloat16 [3072, 64, 576], P('layer'), may hold values from -0.25 to 0.25
- conv_bias: float32 [3072, 64], P('layer'), may hold values from -3 to 3
- coarse_matrix: float32 [64, 64, 64], P('layer'), may hold values from -1 to 1
Outputs:
- block_final_states: float32 [64, 4, 64, 1024], P('layer', 'dp'), parts along dimension 1
- corrected: float32 [64, 4, 64, 1024], P('layer', 'dp'), parts along dimension 1
There are 4 independent parts, one for each index of `dp`. A program takes and returns all parts, laid end to end along the dimension named above; an argument that names none is the same for every part. Nothing has to cross between parts.
All inputs are finite; a program needn't handle non-finite values.
Results may differ from a plain program's by a relative error of at most 0.0085.
Values sent between devices are 32-bit elements; how exact they have to be, the bound alone decides.
A program may use at most 64 MiB of HBM per device.

v0:
```python
import jax
import jax.numpy as jnp
from jax import lax
from jax.sharding import PartitionSpec as P

SIDE = 32


step_size = 0.25


def from_behind(value, axis, steps):
    count = lax.axis_size(axis)
    initial, last = (max(0, -steps), min(count, count - steps))
    return lax.ppermute(value, axis, [(source, source + steps) for source in range(initial, last)])


def unfold_taps(current):
    leading = current.shape[:-1]
    images = current.reshape(leading + (SIDE, SIDE))
    widths = [(0, 0)] * (images.ndim - 2) + [(1, 1), (1, 1)]
    padded = jnp.pad(images, widths)
    pieces = [
        padded[..., row_off : row_off + SIDE, col_off : col_off + SIDE].reshape(current.shape)
        for row_off in range(3)
        for col_off in range(3)
    ]
    return jnp.concatenate(pieces, axis=-2)


def relax_block(start, conv_weight, conv_bias):

    def advance(current, layer_pair):
        current_weight, bias_now = layer_pair
        stacked = unfold_taps(current.astype(jnp.bfloat16))
        mixed = jnp.einsum(
            "oc,icp->iop", current_weight, stacked, preferred_element_type=jnp.float32
        )
        return (current + step_size * jnp.tanh(mixed + bias_now[None, :, None]), None)

    final, unused = lax.scan(advance, start, (conv_weight, conv_bias))
    return final


def apply_matrix(matrix, field):
    return jnp.einsum("cd,idp->icp", matrix, field, precision=lax.Precision.HIGHEST)


def on_device(cpoints, network_input, conv_weight, conv_bias, coarse_matrix):
    start = cpoints[0]
    ends = relax_block(start, conv_weight, conv_bias)
    received, matrix_in = from_behind((ends, coarse_matrix[0]), "layer", 1)
    leading_block = lax.axis_index("layer") == 0
    mismatch_vector = jnp.where(leading_block, network_input - start, received - start)

    def sweep_turn(counter, carried):
        previous = from_behind(carried, "layer", 1)
        return apply_matrix(matrix_in, previous) + mismatch_vector

    correction = lax.fori_loop(0, lax.axis_size("layer") - 1, sweep_turn, mismatch_vector)
    corrected = start + correction
    block_final_states = relax_block(corrected, conv_weight, conv_bias)
    return (block_final_states[None], corrected[None])


def solution(mesh):
    placed = (
        P("layer", "dp", None, None),
        P("dp", None, None),
        P("layer", None, None),
        P("layer", None),
        P("layer", None, None),
    )
    return jax.shard_map(
        on_device,
        mesh=mesh,
        in_specs=placed,
        out_specs=(P("layer", "dp", None, None), P("layer", "dp", None, None)),
        check_vma=False,
    )
```

profile of v0, /device:TPU:14, one launch (start us, length us, event | category | flops | bytes accessed | tf_op | source)
XLA Modules:
  0.0 1221.0 jit_solution(12050709990616818042)
XLA Ops:
  1.6 281.5 %while.34 = (s32[]{:T(128)}, f32[1,64,1024]{2,1,0:T(8,128)S(1)}, bf16[48,64,576]{2,1,0:T(8,128)(2,1)}, f32[48,64]{1,0:T(8,128)}, s32[]{:T(128)}) while((s32[]{:T(128)}, f32[1,64,1024]{2,1,0:T(8,128)S(1)}, bf16[48,64,576]{2,1,0:T(8,128)(2,1)}, f32[48,64]{1,0:T(8,128)}, s32[]{:T(128)}) %tuple.82), condition=%wide.region_1.2_spmd, body=%wide.region_0.1_spmd.sunk | while | flops 75694080 | bytes 5719361 | solution.py:41
  295.8 642.1 %while.35 = (s32[]{:T(128)}, f32[1,64,1024]{2,1,0:T(8,128)S(1)}, f32[64,64]{1,0:T(8,128)S(1)}, f32[1,64,1024]{2,1,0:T(8,128)S(1)}, s32[]{:T(128)}) while((s32[]{:T(128)}, f32[1,64,1024]{2,1,0:T(8,128)S(1)}, f32[64,64]{1,0:T(8,128)S(1)}, f32[1,64,1024]{2,1,0:T(8,128)S(1)}, s32[]{:T(128)}) %tuple.85), condition=%wide.region_3.4_spmd, body=%wide.region_2.3_spmd.sunk | while | flops 50397184 | bytes 1851493 | solution.py:60
  297.8 7.9 collective-permute-done
  308.0 7.9 collective-permute-done
  318.2 7.9 collective-permute-done
  328.4 7.9 collective-permute-done
  338.6 7.9 collective-permute-done
  348.8 7.9 collective-permute-done
  359.0 7.9 collective-permute-done
  369.2 7.9 collective-permute-done
  379.3 7.9 collective-permute-done
  389.5 7.9 collective-permute-done
  399.7 7.9 collective-permute-done
  409.9 7.9 collective-permute-done
  420.1 7.9 collective-permute-done
  430.3 7.9 collective-permute-done
  440.5 7.9 collective-permute-done
  450.7 7.9 collective-permute-done
  460.9 7.9 collective-permute-done
  471.1 7.9 collective-permute-done
  481.2 7.9 collective-permute-done
  491.4 7.9 collective-permute-done
  501.6 7.9 collective-permute-done
  511.8 7.9 collective-permute-done
  522.0 7.9 collective-permute-done
  532.2 7.9 collective-permute-done
  542.4 7.9 collective-permute-done
  552.6 7.9 collective-permute-done
  562.8 7.9 collective-permute-done
  572.9 7.9 collective-permute-done
  583.1 7.9 collective-permute-done
  593.3 7.9 collective-permute-done
  603.5 7.9 collective-permute-done
  613.7 7.9 collective-permute-done
  623.9 7.9 collective-permute-done
  634.1 7.9 collective-permute-done
  644.3 7.9 collective-permute-done
  654.5 7.9 collective-permute-done
  664.7 7.9 collective-permute-done
  674.8 7.9 collective-permute-done
  685.0 7.9 collective-permute-done
  695.2 7.9 collective-permute-done
  705.4 7.9 collective-permute-done
  715.6 7.9 collective-permute-done
  725.8 7.9 collective-permute-done
  736.0 7.9 collective-permute-done
  746.2 7.9 collective-permute-done
  756.4 7.9 collective-permute-done
  766.5 7.9 collective-permute-done
  776.7 7.9 collective-permute-done
  786.9 7.9 collective-permute-done
  797.1 7.9 collective-permute-done
  807.3 7.9 collective-permute-done
  817.5 7.9 collective-permute-done
  827.7 7.9 collective-permute-done
  837.9 7.9 collective-permute-done
  848.1 7.9 collective-permute-done
  858.3 7.9 collective-permute-done
  868.4 7.9 collective-permute-done
  878.6 7.9 collective-permute-done
  888.8 7.9 collective-permute-done
  899.0 7.9 collective-permute-done
  919.4 7.9 collective-permute-done
  938.6 281.7 %while.36 = (s32[]{:T(128)}, f32[1,64,1024]{2,1,0:T(8,128)S(1)}, bf16[48,64,576]{2,1,0:T(8,128)(2,1)}, f32[48,64]{1,0:T(8,128)}, s32[]{:T(128)}) while((s32[]{:T(128)}, f32[1,64,1024]{2,1,0:T(8,128)S(1)}, bf16[48,64,576]{2,1,0:T(8,128)(2,1)}, f32[48,64]{1,0:T(8,128)}, s32[]{:T(128)}) %tuple.92), condition=%wide.region_5.6_spmd, body=%wide.region_4.5_spmd.sunk | while | flops 75694080 | bytes 5719361 | solution.py:41
  (625 shorter events, 734.5 us)
Async XLA Ops:
  283.1 11.5 collective-permute-start.1
  285.1 10.7 collective-permute-start.2
  295.8 9.9 collective-permute-start
  306.1 9.8 collective-permute-start
  316.3 9.8 collective-permute-start
  326.5 9.8 collective-permute-start
  336.7 9.8 collective-permute-start
  346.8 9.8 collective-permute-start
  357.0 9.8 collective-permute-start
  367.2 9.8 collective-permute-start
  377.4 9.8 collective-permute-start
  387.6 9.8 collective-permute-start
  397.8 9.8 collective-permute-start
  408.0 9.8 collective-permute-start
  418.2 9.8 collective-permute-start
  428.4 9.8 collective-permute-start
  438.6 9.8 collective-permute-start
  448.7 9.8 collective-permute-start
  458.9 9.8 collective-permute-start
  469.1 9.8 collective-permute-start
  479.3 9.8 collective-permute-start
  489.5 9.8 collective-permute-start
  499.7 9.8 collective-permute-start
  509.9 9.8 collective-permute-start
  520.1 9.8 collective-permute-start
  530.3 9.8 collective-permute-start
  540.4 9.8 collective-permute-start
  550.6 9.8 collective-permute-start
  560.8 9.8 collective-permute-start
  571.0 9.8 collective-permute-start
  581.2 9.8 collective-permute-start
  591.4 9.8 collective-permute-start
  601.6 9.8 collective-permute-start
  611.8 9.8 collective-permute-start
  622.0 9.8 collective-permute-start
  632.2 9.8 collective-permute-start
  642.3 9.8 collective-permute-start
  652.5 9.8 collective-permute-start
  662.7 9.8 collective-permute-start
  672.9 9.8 collective-permute-start
  683.1 9.8 collective-permute-start
  693.3 9.8 collective-permute-start
  703.5 9.8 collective-permute-start
  713.7 9.8 collective-permute-start
  723.9 9.8 collective-permute-start
  734.0 9.8 collective-permute-start
  744.2 9.8 collective-permute-start
  754.4 9.8 collective-permute-start
  764.6 9.8 collective-permute-start
  774.8 9.8 collective-permute-start
  785.0 9.8 collective-permute-start
  795.2 9.8 collective-permute-start
  805.4 9.8 collective-permute-start
  815.6 9.8 collective-permute-start
  825.8 9.8 collective-permute-start
  835.9 9.8 collective-permute-start
  846.1 9.8 collective-permute-start
  856.3 9.8 collective-permute-start
  866.5 9.8 collective-permute-start
  876.7 9.8 collective-permute-start
  886.9 9.8 collective-permute-start
  897.1 9.8 collective-permute-start
  907.3 9.8 collective-permute-start
  917.5 9.8 collective-permute-start
  (5 other events, 936.8 us)
where the time goes:
time: 1240 us; the launch traced here: 1220 us
  waiting for transfers between devices  502 us (40%)
  local copies, waits for them, and re-layouts  422 us (34%)
  matrix products  163 us (13%)
  starting transfers between devices  127 us (10%)
    ppermute x65, waiting for transfers between devices, from_behind(): lax.ppermute(value, axis, [(source, source + steps) for source in range(i...  502 us
    concatenate x96, local copies, waits for them, and re-layouts, unfold_taps(): return jnp.concatenate(pieces, axis=-2)  229 us
    dot_general x96, matrix products, advance(): jnp.einsum('oc,icp->iop', current_weight, stacked, preferred_element_type...  140 us
    ppermute x65, starting transfers between devices, from_behind(): lax.ppermute(value, axis, [(source, source + steps) for source in range(i...  127 us
    slice x96, local copies, waits for them, and re-layouts, unfold_taps(): padded[..., row_off:row_off + SIDE, col_off:col_off + SIDE]  107 us
    add x96, local copies, waits for them, and re-layouts, advance(): mixed + bias_now[None, :, None]  67 us
  transfers between devices with their start and end apart: 65, of which 64 were waited for; matrix products, arithmetic and copies ran while one was open for 0% of the time, Pallas kernels for 0%

commit v1 on v0

v1 whole, which is shorter than its diff:
```python
import functools
import jax
import jax.numpy as jnp
from jax import lax
from jax.experimental import pallas as pl
from jax.experimental.pallas import tpu as pltpu
from jax.sharding import PartitionSpec as P

SIDE = 32
LANES = 128
step_size = 0.25


def to_bands(tiles):
    group = lax.broadcasted_iota(jnp.int32, tiles[0].shape, 1) // SIDE
    bands = []
    for band in range(8):
        out = None
        for slot in range(4):
            turn = SIDE * ((slot - band) % 4)
            tile = tiles[2 * slot + band // 4]
            tile = pltpu.roll(tile, turn, 1) if turn else tile
            out = tile if out is None else jnp.where(group == slot, tile, out)
        bands.append(out)
    return bands


def from_bands(bands):
    group = lax.broadcasted_iota(jnp.int32, bands[0].shape, 1) // SIDE
    tiles = []
    for tile in range(8):
        out = None
        for slot in range(4):
            turn = SIDE * ((slot - tile // 2) % 4)
            band = bands[4 * (tile % 2) + slot]
            band = pltpu.roll(band, turn, 1) if turn else band
            out = band if out is None else jnp.where(group == slot, band, out)
        tiles.append(out)
    return tiles


def split_lanes(value):
    return [value[:, LANES * k : LANES * (k + 1)] for k in range(value.shape[1] // LANES)]


def conv_layers(state_ref, weight_ref, bias_ref, unroll):
    ch = state_ref.shape[1]
    lane = lax.broadcasted_iota(jnp.int32, (ch, LANES), 1)
    column = lane % SIDE
    not_first, not_last = column != 0, column != SIDE - 1
    below, above = lane >= SIDE, lane < LANES - SIDE

    def layer(index, unused):
        weight = weight_ref[index]
        rows = jnp.concatenate([weight[:, 3 * ch * k : 3 * ch * (k + 1)] for k in range(3)], axis=0)
        bias = bias_ref[index]
        left, mid, right = [], [], []
        for band in range(8):
            value = state_ref[band]
            left.append(jnp.where(not_first, pltpu.roll(value, 1, 1), 0.0).astype(jnp.bfloat16))
            mid.append(value.astype(jnp.bfloat16))
            right.append(jnp.where(not_last, pltpu.roll(value, LANES - 1, 1), 0.0).astype(jnp.bfloat16))
        taps = []
        for pair in range(4):
            stack = jnp.concatenate(
                [jnp.concatenate(part[2 * pair : 2 * pair + 2], axis=1) for part in (left, mid, right)], axis=0
            )
            full = jnp.dot(rows, stack, preferred_element_type=jnp.float32)
            taps += [full[:, :LANES], full[:, LANES:]]
        for band in range(8):
            up = taps[band - 1][:ch]
            if band == 0:
                up = jnp.where(below, pltpu.roll(up, SIDE, 1), 0.0)
            down = taps[(band + 1) % 8][2 * ch :]
            if band == 7:
                down = jnp.where(above, pltpu.roll(down, LANES - SIDE, 1), 0.0)
            mixed = taps[band][ch : 2 * ch] + up + down
            state_ref[band] = state_ref[band] + step_size * jnp.tanh(mixed + bias)
        return unused

    lax.fori_loop(0, weight_ref.shape[0], layer, 0, unroll=unroll)


def block_kernel(start_ref, weight_ref, bias_ref, final_ref, state, unroll=1):
    for band, value in enumerate(to_bands(split_lanes(start_ref[...]))):
        state[band] = value
    conv_layers(state, weight_ref, bias_ref, unroll)
    for tile, value in enumerate(from_bands([state[band] for band in range(8)])):
        final_ref[:, LANES * tile : LANES * (tile + 1)] = value


def relax_block(start, conv_weight, bias_wide, unroll=1):
    ch, pixels = start.shape
    return pl.pallas_call(
        functools.partial(block_kernel, unroll=unroll),
        out_shape=jax.ShapeDtypeStruct((ch, pixels), jnp.float32),
        in_specs=[pl.BlockSpec(memory_space=pltpu.VMEM)] * 3,
        out_specs=pl.BlockSpec(memory_space=pltpu.VMEM),
        scratch_shapes=[pltpu.VMEM((8, ch, LANES), jnp.float32)],
        compiler_params=pltpu.CompilerParams(vmem_limit_bytes=60 << 20),
    )(start, conv_weight, bias_wide)


def from_behind(value, axis, steps):
    count = lax.axis_size(axis)
    initial, last = (max(0, -steps), min(count, count - steps))
    return lax.ppermute(value, axis, [(source, source + steps) for source in range(initial, last)])


def apply_matrix(matrix, field):
    return jnp.einsum("cd,idp->icp", matrix, field, precision=lax.Precision.HIGHEST)


def on_device(cpoints, network_input, conv_weight, conv_bias, coarse_matrix):
    start = cpoints[0]
    bias_wide = jnp.broadcast_to(conv_bias[:, :, None], conv_bias.shape + (LANES,))
    ends = relax_block(start[0], conv_weight, bias_wide)[None]
    received, matrix_in = from_behind((ends, coarse_matrix[0]), "layer", 1)
    leading_block = lax.axis_index("layer") == 0
    mismatch_vector = jnp.where(leading_block, network_input - start, received - start)

    def sweep_turn(counter, carried):
        previous = from_behind(carried, "layer", 1)
        return apply_matrix(matrix_in, previous) + mismatch_vector

    correction = lax.fori_loop(0, lax.axis_size("layer") - 1, sweep_turn, mismatch_vector)
    corrected = start + correction
    block_final_states = relax_block(corrected[0], conv_weight, bias_wide)[None]
    return (block_final_states[None], corrected[None])


def solution(mesh):
    placed = (
        P("layer", "dp", None, None),
        P("dp", None, None),
        P("layer", None, None),
        P("layer", None),
        P("layer", None, None),
    )
    return jax.shard_map(
        on_device,
        mesh=mesh,
        in_specs=placed,
        out_specs=(P("layer", "dp", None, None), P("layer", "dp", None, None)),
        check_vma=False,
    )
```

time: 1240 us -> 706 us (0.57); the launches traced: 1220 us -> 703 us
  local copies, waits for them, and re-layouts: 422 us -> 2.44 us
  matrix products: 163 us -> 23 us
  Pallas kernels: 0 us -> 45 us
    concatenate x96 -> x0, local copies, waits for them, and re-layouts: 229 us -> none  [unfold_taps(): return jnp.concatenate(pieces, axis=-2)]
    dot_general x96 -> x0, matrix products: 140 us -> none  [advance(): jnp.einsum('oc,icp->iop', current_weight, stacked, preferred_element_type...]
    slice x96 -> x0, local copies, waits for them, and re-layouts: 107 us -> none  [unfold_taps(): padded[..., row_off:row_off + SIDE, col_off:col_off + SIDE]]
    add x96 -> x0, local copies, waits for them, and re-layouts: 67 us -> none  [advance(): mixed + bias_now[None, :, None]]
    pallas_call x0 -> x2, Pallas kernels: none -> 45 us  [relax_block(): pl.pallas_call(functools.partial(block_kernel, unroll=unroll), out_shape=...]
    another operation x96 -> x0, local copies, waits for them, and re-layouts: 16.2 us -> none
  transfers between devices with their start and end apart: 65 -> 65, of which waited for: 64 -> 65; matrix products, arithmetic and copies ran while one was open for 0% -> 0% of each run, Pallas kernels for 0% -> 0%
where the time goes in v1:
time: 706 us; the launch traced here: 703 us
  waiting for transfers between devices  502 us (71%)
  starting transfers between devices  127 us (18%)
  Pallas kernels  45 us (6%)
  matrix products  23 us (3%)
    ppermute x65, waiting for transfers between devices, from_behind(): lax.ppermute(value, axis, [(source, source + steps) for source in range(i...  502 us
    ppermute x65, starting transfers between devices, from_behind(): lax.ppermute(value, axis, [(source, source + steps) for source in range(i...  127 us
    pallas_call x2, Pallas kernels, relax_block(): pl.pallas_call(functools.partial(block_kernel, unroll=unroll), out_shape=...  45 us
    dot_general x63, matrix products, apply_matrix(): jnp.einsum('cd,idp->icp', matrix, field, precision=lax.Precision.HIGHEST)  23 us
  transfers between devices with their start and end apart: 65, of which 65 were waited for; matrix products, arithmetic and copies ran while one was open for 0% of the time, Pallas kernels for 0%

profile of v1, /device:TPU:14, one launch (start us, length us, event | category | flops | bytes accessed | tf_op | source)
XLA Modules:
  0.0 702.9 jit_solution(12732835142601047695)
XLA Ops:
  3.1 22.5 %shard_map.68 = f32[64,1024]{1,0:T(8,128)} custom-call(f32[64,1024]{1,0:T(8,128)} %bitcast.36, bf16[48,64,576]{2,1,0:T(8,128)(2,1)} %weight_ref.3, f32[48,64,128]{2,1,0:T(8,128)} %broadcast_in_dim.12.bias_ref), custom_call_target="tpu_custom_call" | custom-call | tf_op jit(solution)/shard_map/pallas_call | solution.py:94
  37.6 641.9 %while.10 = (s32[]{:T(128)}, f32[1,64,1024]{2,1,0:T(8,128)S(1)}, f32[64,64]{1,0:T(8,128)S(1)}, f32[1,64,1024]{2,1,0:T(8,128)S(1)}, s32[]{:T(128)}) while((s32[]{:T(128)}, f32[1,64,1024]{2,1,0:T(8,128)S(1)}, f32[64,64]{1,0:T(8,128)S(1)}, f32[1,64,1024]{2,1,0:T(8,128)S(1)}, s32[]{:T(128)}) %tuple.23), condition=%wide.region_1.2_spmd, body=%wide.region_0.1_spmd.sunk | while | flops 50397184 | bytes 1851493 | solution.py:126
  39.6 7.9 %collective-permute-done = f32[1,64,1024]{2,1,0:T(8,128)S(1)} collective-permute-done((f32[1,64,1024]{2,1,0:T(8,128)S(1)}, f32[1,64,1024]{2,1,0:T(8,128)S(1)}, u32[]{:S(2)}, u32[]{:S(2)}) %collective-permute-start) | collective-permute-done | bytes 262176 | tf_op jit(solution)/shard_map/while/body/eval_jaxpr/ppermute | solution.py:107
  49.7 7.9 %collective-permute-done = f32[1,64,1024]{2,1,0:T(8,128)S(1)} collective-permute-done((f32[1,64,1024]{2,1,0:T(8,128)S(1)}, f32[1,64,1024]{2,1,0:T(8,128)S(1)}, u32[]{:S(2)}, u32[]{:S(2)}) %collective-permute-start) | collective-permute-done | bytes 262176 | tf_op jit(solution)/shard_map/while/body/eval_jaxpr/ppermute | solution.py:107
  59.9 7.9 %collective-permute-done = f32[1,64,1024]{2,1,0:T(8,128)S(1)} collective-permute-done((f32[1,64,1024]{2,1,0:T(8,128)S(1)}, f32[1,64,1024]{2,1,0:T(8,128)S(1)}, u32[]{:S(2)}, u32[]{:S(2)}) %collective-permute-start) | collective-permute-done | bytes 262176 | tf_op jit(solution)/shard_map/while/body/eval_jaxpr/ppermute | solution.py:107
  70.1 7.9 %collective-permute-done = f32[1,64,1024]{2,1,0:T(8,128)S(1)} collective-permute-done((f32[1,64,1024]{2,1,0:T(8,128)S(1)}, f32[1,64,1024]{2,1,0:T(8,128)S(1)}, u32[]{:S(2)}, u32[]{:S(2)}) %collective-permute-start) | collective-permute-done | bytes 262176 | tf_op jit(solution)/shard_map/while/body/eval_jaxpr/ppermute | solution.py:107
  80.3 7.9 %collective-permute-done = f32[1,64,1024]{2,1,0:T(8,128)S(1)} collective-permute-done((f32[1,64,1024]{2,1,0:T(8,128)S(1)}, f32[1,64,1024]{2,1,0:T(8,128)S(1)}, u32[]{:S(2)}, u32[]{:S(2)}) %collective-permute-start) | collective-permute-done | bytes 262176 | tf_op jit(solution)/shard_map/while/body/eval_jaxpr/ppermute | solution.py:107
  90.5 7.9 %collective-permute-done = f32[1,64,1024]{2,1,0:T(8,128)S(1)} collective-permute-done((f32[1,64,1024]{2,1,0:T(8,128)S(1)}, f32[1,64,1024]{2,1,0:T(8,128)S(1)}, u32[]{:S(2)}, u32[]{:S(2)}) %collective-permute-start) | collective-permute-done | bytes 262176 | tf_op jit(solution)/shard_map/while/body/eval_jaxpr/ppermute | solution.py:107
  100.7 7.9 %collective-permute-done = f32[1,64,1024]{2,1,0:T(8,128)S(1)} collective-permute-done((f32[1,64,1024]{2,1,0:T(8,128)S(1)}, f32[1,64,1024]{2,1,0:T(8,128)S(1)}, u32[]{:S(2)}, u32[]{:S(2)}) %collective-permute-start) | collective-permute-done | bytes 262176 | tf_op jit(solution)/shard_map/while/body/eval_jaxpr/ppermute | solution.py:107
  110.9 7.9 %collective-permute-done = f32[1,64,1024]{2,1,0:T(8,128)S(1)} collective-permute-done((f32[1,64,1024]{2,1,0:T(8,128)S(1)}, f32[1,64,1024]{2,1,0:T(8,128)S(1)}, u32[]{:S(2)}, u32[]{:S(2)}) %collective-permute-start) | collective-permute-done | bytes 262176 | tf_op jit(solution)/shard_map/while/body/eval_jaxpr/ppermute | solution.py:107
  121.1 7.9 %collective-permute-done = f32[1,64,1024]{2,1,0:T(8,128)S(1)} collective-permute-done((f32[1,64,1024]{2,1,0:T(8,128)S(1)}, f32[1,64,1024]{2,1,0:T(8,128)S(1)}, u32[]{:S(2)}, u32[]{:S(2)}) %collective-permute-start) | collective-permute-done | bytes 262176 | tf_op jit(solution)/shard_map/while/body/eval_jaxpr/ppermute | solution.py:107
  131.3 7.9 %collective-permute-done = f32[1,64,1024]{2,1,0:T(8,128)S(1)} collective-permute-done((f32[1,64,1024]{2,1,0:T(8,128)S(1)}, f32[1,64,1024]{2,1,0:T(8,128)S(1)}, u32[]{:S(2)}, u32[]{:S(2)}) %collective-permute-start) | collective-permute-done | bytes 262176 | tf_op jit(solution)/shard_map/while/body/eval_jaxpr/ppermute | solution.py:107
  141.4 7.9 %collective-permute-done = f32[1,64,1024]{2,1,0:T(8,128)S(1)} collective-permute-done((f32[1,64,1024]{2,1,0:T(8,128)S(1)}, f32[1,64,1024]{2,1,0:T(8,128)S(1)}, u32[]{:S(2)}, u32[]{:S(2)}) %collective-permute-start) | collective-permute-done | bytes 262176 | tf_op jit(solution)/shard_map/while/body/eval_jaxpr/ppermute | solution.py:107
  151.6 7.9 %collective-permute-done = f32[1,64,1024]{2,1,0:T(8,128)S(1)} collective-permute-done((f32[1,64,1024]{2,1,0:T(8,128)S(1)}, f32[1,64,1024]{2,1,0:T(8,128)S(1)}, u32[]{:S(2)}, u32[]{:S(2)}) %collective-permute-start) | collective-permute-done | bytes 262176 | tf_op jit(solution)/shard_map/while/body/eval_jaxpr/ppermute | solution.py:107
  161.8 7.9 %collective-permute-done = f32[1,64,1024]{2,1,0:T(8,128)S(1)} collective-permute-done((f32[1,64,1024]{2,1,0:T(8,128)S(1)}, f32[1,64,1024]{2,1,0:T(8,128)S(1)}, u32[]{:S(2)}, u32[]{:S(2)}) %collective-permute-start) | collective-permute-done | bytes 262176 | tf_op jit(solution)/shard_map/while/body/eval_jaxpr/ppermute | solution.py:107
  172.0 7.9 %collective-permute-done = f32[1,64,1024]{2,1,0:T(8,128)S(1)} collective-permute-done((f32[1,64,1024]{2,1,0:T(8,128)S(1)}, f32[1,64,1024]{2,1,0:T(8,128)S(1)}, u32[]{:S(2)}, u32[]{:S(2)}) %collective-permute-start) | collective-permute-done | bytes 262176 | tf_op jit(solution)/shard_map/while/body/eval_jaxpr/ppermute | solution.py:107
  182.2 7.9 %collective-permute-done = f32[1,64,1024]{2,1,0:T(8,128)S(1)} collective-permute-done((f32[1,64,1024]{2,1,0:T(8,128)S(1)}, f32[1,64,1024]{2,1,0:T(8,128)S(1)}, u32[]{:S(2)}, u32[]{:S(2)}) %collective-permute-start) | collective-permute-done | bytes 262176 | tf_op jit(solution)/shard_map/while/body/eval_jaxpr/ppermute | solution.py:107
  192.4 7.9 %collective-permute-done = f32[1,64,1024]{2,1,0:T(8,128)S(1)} collective-permute-done((f32[1,64,1024]{2,1,0:T(8,128)S(1)}, f32[1,64,1024]{2,1,0:T(8,128)S(1)}, u32[]{:S(2)}, u32[]{:S(2)}) %collective-permute-start) | collective-permute-done | bytes 262176 | tf_op jit(solution)/shard_map/while/body/eval_jaxpr/ppermute | solution.py:107
  202.6 7.9 %collective-permute-done = f32[1,64,1024]{2,1,0:T(8,128)S(1)} collective-permute-done((f32[1,64,1024]{2,1,0:T(8,128)S(1)}, f32[1,64,1024]{2,1,0:T(8,128)S(1)}, u32[]{:S(2)}, u32[]{:S(2)}) %collective-permute-start) | collective-permute-done | bytes 262176 | tf_op jit(solution)/shard_map/while/body/eval_jaxpr/ppermute | solution.py:107
  212.8 7.9 %collective-permute-done = f32[1,64,1024]{2,1,0:T(8,128)S(1)} collective-permute-done((f32[1,64,1024]{2,1,0:T(8,128)S(1)}, f32[1,64,1024]{2,1,0:T(8,128)S(1)}, u32[]{:S(2)}, u32[]{:S(2)}) %collective-permute-start) | collective-permute-done | bytes 262176 | tf_op jit(solution)/shard_map/while/body/eval_jaxpr/ppermute | solution.py:107
  223.0 7.9 %collective-permute-done = f32[1,64,1024]{2,1,0:T(8,128)S(1)} collective-permute-done((f32[1,64,1024]{2,1,0:T(8,128)S(1)}, f32[1,64,1024]{2,1,0:T(8,128)S(1)}, u32[]{:S(2)}, u32[]{:S(2)}) %collective-permute-start) | collective-permute-done | bytes 262176 | tf_op jit(solution)/shard_map/while/body/eval_jaxpr/ppermute | solution.py:107
  233.2 7.9 %collective-permute-done = f32[1,64,1024]{2,1,0:T(8,128)S(1)} collective-permute-done((f32[1,64,1024]{2,1,0:T(8,128)S(1)}, f32[1,64,1024]{2,1,0:T(8,128)S(1)}, u32[]{:S(2)}, u32[]{:S(2)}) %collective-permute-start) | collective-permute-done | bytes 262176 | tf_op jit(solution)/shard_map/while/body/eval_jaxpr/ppermute | solution.py:107
  243.3 7.9 %collective-permute-done = f32[1,64,1024]{2,1,0:T(8,128)S(1)} collective-permute-done((f32[1,64,1024]{2,1,0:T(8,128)S(1)}, f32[1,64,1024]{2,1,0:T(8,128)S(1)}, u32[]{:S(2)}, u32[]{:S(2)}) %collective-permute-start) | collective-permute-done | bytes 262176 | tf_op jit(solution)/shard_map/while/body/eval_jaxpr/ppermute | solution.py:107
  253.5 7.9 %collective-permute-done = f32[1,64,1024]{2,1,0:T(8,128)S(1)} collective-permute-done((f32[1,64,1024]{2,1,0:T(8,128)S(1)}, f32[1,64,1024]{2,1,0:T(8,128)S(1)}, u32[]{:S(2)}, u32[]{:S(2)}) %collective-permute-start) | collective-permute-done | bytes 262176 | tf_op jit(solution)/shard_map/while/body/eval_jaxpr/ppermute | solution.py:107
  263.7 7.9 %collective-permute-done = f32[1,64,1024]{2,1,0:T(8,128)S(1)} collective-permute-done((f32[1,64,1024]{2,1,0:T(8,128)S(1)}, f32[1,64,1024]{2,1,0:T(8,128)S(1)}, u32[]{:S(2)}, u32[]{:S(2)}) %collective-permute-start) | collective-permute-done | bytes 262176 | tf_op jit(solution)/shard_map/while/body/eval_jaxpr/ppermute | solution.py:107
  273.9 7.9 %collective-permute-done = f32[1,64,1024]{2,1,0:T(8,128)S(1)} collective-permute-done((f32[1,64,1024]{2,1,0:T(8,128)S(1)}, f32[1,64,1024]{2,1,0:T(8,128)S(1)}, u32[]{:S(2)}, u32[]{:S(2)}) %collective-permute-start) | collective-permute-done | bytes 262176 | tf_op jit(solution)/shard_map/while/body/eval_jaxpr/ppermute | solution.py:107
  284.1 7.9 %collective-permute-done = f32[1,64,1024]{2,1,0:T(8,128)S(1)} collective-permute-done((f32[1,64,1024]{2,1,0:T(8,128)S(1)}, f32[1,64,1024]{2,1,0:T(8,128)S(1)}, u32[]{:S(2)}, u32[]{:S(2)}) %collective-permute-start) | collective-permute-done | bytes 262176 | tf_op jit(solution)/shard_map/while/body/eval_jaxpr/ppermute | solution.py:107
  294.3 7.9 %collective-permute-done = f32[1,64,1024]{2,1,0:T(8,128)S(1)} collective-permute-done((f32[1,64,1024]{2,1,0:T(8,128)S(1)}, f32[1,64,1024]{2,1,0:T(8,128)S(1)}, u32[]{:S(2)}, u32[]{:S(2)}) %collective-permute-start) | collective-permute-done | bytes 262176 | tf_op jit(solution)/shard_map/while/body/eval_jaxpr/ppermute | solution.py:107
  304.5 7.9 %collective-permute-done = f32[1,64,1024]{2,1,0:T(8,128)S(1)} collective-permute-done((f32[1,64,1024]{2,1,0:T(8,128)S(1)}, f32[1,64,1024]{2,1,0:T(8,128)S(1)}, u32[]{:S(2)}, u32[]{:S(2)}) %collective-permute-start) | collective-permute-done | bytes 262176 | tf_op jit(solution)/shard_map/while/body/eval_jaxpr/ppermute | solution.py:107
  314.7 7.9 %collective-permute-done = f32[1,64,1024]{2,1,0:T(8,128)S(1)} collective-permute-done((f32[1,64,1024]{2,1,0:T(8,128)S(1)}, f32[1,64,1024]{2,1,0:T(8,128)S(1)}, u32[]{:S(2)}, u32[]{:S(2)}) %collective-permute-start) | collective-permute-done | bytes 262176 | tf_op jit(solution)/shard_map/while/body/eval_jaxpr/ppermute | solution.py:107
  324.9 7.9 %collective-permute-done = f32[1,64,1024]{2,1,0:T(8,128)S(1)} collective-permute-done((f32[1,64,1024]{2,1,0:T(8,128)S(1)}, f32[1,64,1024]{2,1,0:T(8,128)S(1)}, u32[]{:S(2)}, u32[]{:S(2)}) %collective-permute-start) | collective-permute-done | bytes 262176 | tf_op jit(solution)/shard_map/while/body/eval_jaxpr/ppermute | solution.py:107
  335.0 7.9 %collective-permute-done = f32[1,64,1024]{2,1,0:T(8,128)S(1)} collective-permute-done((f32[1,64,1024]{2,1,0:T(8,128)S(1)}, f32[1,64,1024]{2,1,0:T(8,128)S(1)}, u32[]{:S(2)}, u32[]{:S(2)}) %collective-permute-start) | collective-permute-done | bytes 262176 | tf_op jit(solution)/shard_map/while/body/eval_jaxpr/ppermute | solution.py:107
  345.2 7.9 %collective-permute-done = f32[1,64,1024]{2,1,0:T(8,128)S(1)} collective-permute-done((f32[1,64,1024]{2,1,0:T(8,128)S(1)}, f32[1,64,1024]{2,1,0:T(8,128)S(1)}, u32[]{:S(2)}, u32[]{:S(2)}) %collective-permute-start) | collective-permute-done | bytes 262176 | tf_op jit(solution)/shard_map/while/body/eval_jaxpr/ppermute | solution.py:107
  355.4 7.9 %collective-permute-done = f32[1,64,1024]{2,1,0:T(8,128)S(1)} collective-permute-done((f32[1,64,1024]{2,1,0:T(8,128)S(1)}, f32[1,64,1024]{2,1,0:T(8,128)S(1)}, u32[]{:S(2)}, u32[]{:S(2)}) %collective-permute-start) | collective-permute-done | bytes 262176 | tf_op jit(solution)/shard_map/while/body/eval_jaxpr/ppermute | solution.py:107
  365.6 7.9 %collective-permute-done = f32[1,64,1024]{2,1,0:T(8,128)S(1)} collective-permute-done((f32[1,64,1024]{2,1,0:T(8,128)S(1)}, f32[1,64,1024]{2,1,0:T(8,128)S(1)}, u32[]{:S(2)}, u32[]{:S(2)}) %collective-permute-start) | collective-permute-done | bytes 262176 | tf_op jit(solution)/shard_map/while/body/eval_jaxpr/ppermute | solution.py:107
  375.8 7.9 %collective-permute-done = f32[1,64,1024]{2,1,0:T(8,128)S(1)} collective-permute-done((f32[1,64,1024]{2,1,0:T(8,128)S(1)}, f32[1,64,1024]{2,1,0:T(8,128)S(1)}, u32[]{:S(2)}, u32[]{:S(2)}) %collective-permute-start) | collective-permute-done | bytes 262176 | tf_op jit(solution)/shard_map/while/body/eval_jaxpr/ppermute | solution.py:107
  386.0 7.9 %collective-permute-done = f32[1,64,1024]{2,1,0:T(8,128)S(1)} collective-permute-done((f32[1,64,1024]{2,1,0:T(8,128)S(1)}, f32[1,64,1024]{2,1,0:T(8,128)S(1)}, u32[]{:S(2)}, u32[]{:S(2)}) %collective-permute-start) | collective-permute-done | bytes 262176 | tf_op jit(solution)/shard_map/while/body/eval_jaxpr/ppermute | solution.py:107
  396.2 7.9 %collective-permute-done = f32[1,64,1024]{2,1,0:T(8,128)S(1)} collective-permute-done((f32[1,64,1024]{2,1,0:T(8,128)S(1)}, f32[1,64,1024]{2,1,0:T(8,128)S(1)}, u32[]{:S(2)}, u32[]{:S(2)}) %collective-permute-start) | collective-permute-done | bytes 262176 | tf_op jit(solution)/shard_map/while/body/eval_jaxpr/ppermute | solution.py:107
  406.4 7.9 %collective-permute-done = f32[1,64,1024]{2,1,0:T(8,128)S(1)} collective-permute-done((f32[1,64,1024]{2,1,0:T(8,128)S(1)}, f32[1,64,1024]{2,1,0:T(8,128)S(1)}, u32[]{:S(2)}, u32[]{:S(2)}) %collective-permute-start) | collective-permute-done | bytes 262176 | tf_op jit(solution)/shard_map/while/body/eval_jaxpr/ppermute | solution.py:107
  416.6 7.9 %collective-permute-done = f32[1,64,1024]{2,1,0:T(8,128)S(1)} collective-permute-done((f32[1,64,1024]{2,1,0:T(8,128)S(1)}, f32[1,64,1024]{2,1,0:T(8,128)S(1)}, u32[]{:S(2)}, u32[]{:S(2)}) %collective-permute-start) | collective-permute-done | bytes 262176 | tf_op jit(solution)/shard_map/while/body/eval_jaxpr/ppermute | solution.py:107
  426.8 7.9 %collective-permute-done = f32[1,64,1024]{2,1,0:T(8,128)S(1)} collective-permute-done((f32[1,64,1024]{2,1,0:T(8,128)S(1)}, f32[1,64,1024]{2,1,0:T(8,128)S(1)}, u32[]{:S(2)}, u32[]{:S(2)}) %collective-permute-start) | collective-permute-done | bytes 262176 | tf_op jit(solution)/shard_map/while/body/eval_jaxpr/ppermute | solution.py:107
  436.9 7.9 %collective-permute-done = f32[1,64,1024]{2,1,0:T(8,128)S(1)} collective-permute-done((f32[1,64,1024]{2,1,0:T(8,128)S(1)}, f32[1,64,1024]{2,1,0:T(8,128)S(1)}, u32[]{:S(2)}, u32[]{:S(2)}) %collective-permute-start) | collective-permute-done | bytes 262176 | tf_op jit(solution)/shard_map/while/body/eval_jaxpr/ppermute | solution.py:107
  447.1 7.9 %collective-permute-done = f32[1,64,1024]{2,1,0:T(8,128)S(1)} collective-permute-done((f32[1,64,1024]{2,1,0:T(8,128)S(1)}, f32[1,64,1024]{2,1,0:T(8,128)S(1)}, u32[]{:S(2)}, u32[]{:S(2)}) %collective-permute-start) | collective-permute-done | bytes 262176 | tf_op jit(solution)/shard_map/while/body/eval_jaxpr/ppermute | solution.py:107
  457.3 7.9 %collective-permute-done = f32[1,64,1024]{2,1,0:T(8,128)S(1)} collective-permute-done((f32[1,64,1024]{2,1,0:T(8,128)S(1)}, f32[1,64,1024]{2,1,0:T(8,128)S(1)}, u32[]{:S(2)}, u32[]{:S(2)}) %collective-permute-start) | collective-permute-done | bytes 262176 | tf_op jit(solution)/shard_map/while/body/eval_jaxpr/ppermute | solution.py:107
  467.5 7.9 %collective-permute-done = f32[1,64,1024]{2,1,0:T(8,128)S(1)} collective-permute-done((f32[1,64,1024]{2,1,0:T(8,128)S(1)}, f32[1,64,1024]{2,1,0:T(8,128)S(1)}, u32[]{:S(2)}, u32[]{:S(2)}) %collective-permute-start) | collective-permute-done | bytes 262176 | tf_op jit(solution)/shard_map/while/body/eval_jaxpr/ppermute | solution.py:107
  477.7 7.9 %collective-permute-done = f32[1,64,1024]{2,1,0:T(8,128)S(1)} collective-permute-done((f32[1,64,1024]{2,1,0:T(8,128)S(1)}, f32[1,64,1024]{2,1,0:T(8,128)S(1)}, u32[]{:S(2)}, u32[]{:S(2)}) %collective-permute-start) | collective-permute-done | bytes 262176 | tf_op jit(solution)/shard_map/while/body/eval_jaxpr/ppermute | solution.py:107
  487.9 7.9 %collective-permute-done = f32[1,64,1024]{2,1,0:T(8,128)S(1)} collective-permute-done((f32[1,64,1024]{2,1,0:T(8,128)S(1)}, f32[1,64,1024]{2,1,0:T(8,128)S(1)}, u32[]{:S(2)}, u32[]{:S(2)}) %collective-permute-start) | collective-permute-done | bytes 262176 | tf_op jit(solution)/shard_map/while/body/eval_jaxpr/ppermute | solution.py:107
  498.1 7.9 %collective-permute-done = f32[1,64,1024]{2,1,0:T(8,128)S(1)} collective-permute-done((f32[1,64,1024]{2,1,0:T(8,128)S(1)}, f32[1,64,1024]{2,1,0:T(8,128)S(1)}, u32[]{:S(2)}, u32[]{:S(2)}) %collective-permute-start) | collective-permute-done | bytes 262176 | tf_op jit(solution)/shard_map/while/body/eval_jaxpr/ppermute | solution.py:107
  508.3 7.9 %collective-permute-done = f32[1,64,1024]{2,1,0:T(8,128)S(1)} collective-permute-done((f32[1,64,1024]{2,1,0:T(8,128)S(1)}, f32[1,64,1024]{2,1,0:T(8,128)S(1)}, u32[]{:S(2)}, u32[]{:S(2)}) %collective-permute-start) | collective-permute-done | bytes 262176 | tf_op jit(solution)/shard_map/while/body/eval_jaxpr/ppermute | solution.py:107
  518.5 7.9 %collective-permute-done = f32[1,64,1024]{2,1,0:T(8,128)S(1)} collective-permute-done((f32[1,64,1024]{2,1,0:T(8,128)S(1)}, f32[1,64,1024]{2,1,0:T(8,128)S(1)}, u32[]{:S(2)}, u32[]{:S(2)}) %collective-permute-start) | collective-permute-done | bytes 262176 | tf_op jit(solution)/shard_map/while/body/eval_jaxpr/ppermute | solution.py:107
  528.6 7.9 %collective-permute-done = f32[1,64,1024]{2,1,0:T(8,128)S(1)} collective-permute-done((f32[1,64,1024]{2,1,0:T(8,128)S(1)}, f32[1,64,1024]{2,1,0:T(8,128)S(1)}, u32[]{:S(2)}, u32[]{:S(2)}) %collective-permute-start) | collective-permute-done | bytes 262176 | tf_op jit(solution)/shard_map/while/body/eval_jaxpr/ppermute | solution.py:107
  538.8 7.9 %collective-permute-done = f32[1,64,1024]{2,1,0:T(8,128)S(1)} collective-permute-done((f32[1,64,1024]{2,1,0:T(8,128)S(1)}, f32[1,64,1024]{2,1,0:T(8,128)S(1)}, u32[]{:S(2)}, u32[]{:S(2)}) %collective-permute-start) | collective-permute-done | bytes 262176 | tf_op jit(solution)/shard_map/while/body/eval_jaxpr/ppermute | solution.py:107
  549.0 7.9 %collective-permute-done = f32[1,64,1024]{2,1,0:T(8,128)S(1)} collective-permute-done((f32[1,64,1024]{2,1,0:T(8,128)S(1)}, f32[1,64,1024]{2,1,0:T(8,128)S(1)}, u32[]{:S(2)}, u32[]{:S(2)}) %collective-permute-start) | collective-permute-done | bytes 262176 | tf_op jit(solution)/shard_map/while/body/eval_jaxpr/ppermute | solution.py:107
  559.2 7.9 %collective-permute-done = f32[1,64,1024]{2,1,0:T(8,128)S(1)} collective-permute-done((f32[1,64,1024]{2,1,0:T(8,128)S(1)}, f32[1,64,1024]{2,1,0:T(8,128)S(1)}, u32[]{:S(2)}, u32[]{:S(2)}) %collective-permute-start) | collective-permute-done | bytes 262176 | tf_op jit(solution)/shard_map/while/body/eval_jaxpr/ppermute | solution.py:107
  569.4 7.9 %collective-permute-done = f32[1,64,1024]{2,1,0:T(8,128)S(1)} collective-permute-done((f32[1,64,1024]{2,1,0:T(8,128)S(1)}, f32[1,64,1024]{2,1,0:T(8,128)S(1)}, u32[]{:S(2)}, u32[]{:S(2)}) %collective-permute-start) | collective-permute-done | bytes 262176 | tf_op jit(solution)/shard_map/while/body/eval_jaxpr/ppermute | solution.py:107
  579.6 7.9 %collective-permute-done = f32[1,64,1024]{2,1,0:T(8,128)S(1)} collective-permute-done((f32[1,64,1024]{2,1,0:T(8,128)S(1)}, f32[1,64,1024]{2,1,0:T(8,128)S(1)}, u32[]{:S(2)}, u32[]{:S(2)}) %collective-permute-start) | collective-permute-done | bytes 262176 | tf_op jit(solution)/shard_map/while/body/eval_jaxpr/ppermute | solution.py:107
  589.8 7.9 %collective-permute-done = f32[1,64,1024]{2,1,0:T(8,128)S(1)} collective-permute-done((f32[1,64,1024]{2,1,0:T(8,128)S(1)}, f32[1,64,1024]{2,1,0:T(8,128)S(1)}, u32[]{:S(2)}, u32[]{:S(2)}) %collective-permute-start) | collective-permute-done | bytes 262176 | tf_op jit(solution)/shard_map/while/body/eval_jaxpr/ppermute | solution.py:107
  600.0 7.9 %collective-permute-done = f32[1,64,1024]{2,1,0:T(8,128)S(1)} collective-permute-done((f32[1,64,1024]{2,1,0:T(8,128)S(1)}, f32[1,64,1024]{2,1,0:T(8,128)S(1)}, u32[]{:S(2)}, u32[]{:S(2)}) %collective-permute-start) | collective-permute-done | bytes 262176 | tf_op jit(solution)/shard_map/while/body/eval_jaxpr/ppermute | solution.py:107
  610.2 7.9 %collective-permute-done = f32[1,64,1024]{2,1,0:T(8,128)S(1)} collective-permute-done((f32[1,64,1024]{2,1,0:T(8,128)S(1)}, f32[1,64,1024]{2,1,0:T(8,128)S(1)}, u32[]{:S(2)}, u32[]{:S(2)}) %collective-permute-start) | collective-permute-done | bytes 262176 | tf_op jit(solution)/shard_map/while/body/eval_jaxpr/ppermute | solution.py:107
  620.4 7.9 %collective-permute-done = f32[1,64,1024]{2,1,0:T(8,128)S(1)} collective-permute-done((f32[1,64,1024]{2,1,0:T(8,128)S(1)}, f32[1,64,1024]{2,1,0:T(8,128)S(1)}, u32[]{:S(2)}, u32[]{:S(2)}) %collective-permute-start) | collective-permute-done | bytes 262176 | tf_op jit(solution)/shard_map/while/body/eval_jaxpr/ppermute | solution.py:107
  630.5 7.9 %collective-permute-done = f32[1,64,1024]{2,1,0:T(8,128)S(1)} collective-permute-done((f32[1,64,1024]{2,1,0:T(8,128)S(1)}, f32[1,64,1024]{2,1,0:T(8,128)S(1)}, u32[]{:S(2)}, u32[]{:S(2)}) %collective-permute-start) | collective-permute-done | bytes 262176 | tf_op jit(solution)/shard_map/while/body/eval_jaxpr/ppermute | solution.py:107
  640.7 7.9 %collective-permute-done = f32[1,64,1024]{2,1,0:T(8,128)S(1)} collective-permute-done((f32[1,64,1024]{2,1,0:T(8,128)S(1)}, f32[1,64,1024]{2,1,0:T(8,128)S(1)}, u32[]{:S(2)}, u32[]{:S(2)}) %collective-permute-start) | collective-permute-done | bytes 262176 | tf_op jit(solution)/shard_map/while/body/eval_jaxpr/ppermute | solution.py:107
  661.1 7.9 %collective-permute-done = f32[1,64,1024]{2,1,0:T(8,128)S(1)} collective-permute-done((f32[1,64,1024]{2,1,0:T(8,128)S(1)}, f32[1,64,1024]{2,1,0:T(8,128)S(1)}, u32[]{:S(2)}, u32[]{:S(2)}) %collective-permute-start) | collective-permute-done | bytes 262176 | tf_op jit(solution)/shard_map/while/body/eval_jaxpr/ppermute | solution.py:107
  680.4 22.5 %shard_map.69 = f32[64,1024]{1,0:T(8,128)} custom-call(f32[64,1024]{1,0:T(8,128)} %get-tuple-element.34.start_ref, bf16[48,64,576]{2,1,0:T(8,128)(2,1)} %weight_ref.3, f32[48,64,128]{2,1,0:T(8,128)} %broadcast_in_dim.12.bias_ref), custom_call_target="tpu_custom_call" | custom-call | tf_op jit(solution)/shard_map/pallas_call | solution.py:94
  (142 shorter events, 175.0 us)
Async XLA Ops:
  25.6 11.7 %collective-permute-start.1 = (f32[1,64,1024]{2,1,0:T(8,128)}, f32[1,64,1024]{2,1,0:T(8,128)S(1)}, u32[]{:S(2)}, u32[]{:S(2)}) collective-permute-start(f32[1,64,1024]{2,1,0:T(8,128)} %bitcast.37), channel_id=1, source_target_pairs={{0,4},{4,8},{8,12},{12,16},{16,20},{20,24},{24,28},{28,32},{32,36}... | collective-permute-start | bytes 786440 | tf_op jit(solution)/shard_map/ppermute | solution.py:107
  27.5 10.1 %collective-permute-start.2 = (f32[64,64]{1,0:T(8,128)S(1)}, f32[64,64]{1,0:T(8,128)S(1)}, u32[]{:S(2)}, u32[]{:S(2)}) collective-permute-start(f32[64,64]{1,0:T(8,128)S(1)} %bitcast.39), channel_id=1, source_target_pairs={{0,4},{4,8},{8,12},{12,16},{16,20},{20,24},{24,28},{28,32},{32,36}... | collective-permute-start | bytes 49160 | tf_op jit(solution)/shard_map/ppermute | solution.py:107
  47.8 9.8 %collective-permute-start = (f32[1,64,1024]{2,1,0:T(8,128)S(1)}, f32[1,64,1024]{2,1,0:T(8,128)S(1)}, u32[]{:S(2)}, u32[]{:S(2)}) collective-permute-start(f32[1,64,1024]{2,1,0:T(8,128)S(1)} %get-tuple-element.66), channel_id=1, source_target_pairs={{0,4},{4,8},{8,12},{12,16},{16,20},{20,24},{24,28},{28,32},{32,36}... | collective-permute-start | bytes 786440 | tf_op jit(solution)/shard_map/while/body/eval_jaxpr/ppermute | solution.py:107
  58.0 9.8 %collective-permute-start = (f32[1,64,1024]{2,1,0:T(8,128)S(1)}, f32[1,64,1024]{2,1,0:T(8,128)S(1)}, u32[]{:S(2)}, u32[]{:S(2)}) collective-permute-start(f32[1,64,1024]{2,1,0:T(8,128)S(1)} %get-tuple-element.66), channel_id=1, source_target_pairs={{0,4},{4,8},{8,12},{12,16},{16,20},{20,24},{24,28},{28,32},{32,36}... | collective-permute-start | bytes 786440 | tf_op jit(solution)/shard_map/while/body/eval_jaxpr/ppermute | solution.py:107
  68.2 9.8 %collective-permute-start = (f32[1,64,1024]{2,1,0:T(8,128)S(1)}, f32[1,64,1024]{2,1,0:T(8,128)S(1)}, u32[]{:S(2)}, u32[]{:S(2)}) collective-permute-start(f32[1,64,1024]{2,1,0:T(8,128)S(1)} %get-tuple-element.66), channel_id=1, source_target_pairs={{0,4},{4,8},{8,12},{12,16},{16,20},{20,24},{24,28},{28,32},{32,36}... | collective-permute-start | bytes 786440 | tf_op jit(solution)/shard_map/while/body/eval_jaxpr/ppermute | solution.py:107
  78.4 9.8 %collective-permute-start = (f32[1,64,1024]{2,1,0:T(8,128)S(1)}, f32[1,64,1024]{2,1,0:T(8,128)S(1)}, u32[]{:S(2)}, u32[]{:S(2)}) collective-permute-start(f32[1,64,1024]{2,1,0:T(8,128)S(1)} %get-tuple-element.66), channel_id=1, source_target_pairs={{0,4},{4,8},{8,12},{12,16},{16,20},{20,24},{24,28},{28,32},{32,36}... | collective-permute-start | bytes 786440 | tf_op jit(solution)/shard_map/while/body/eval_jaxpr/ppermute | solution.py:107
  88.6 9.8 %collective-permute-start = (f32[1,64,1024]{2,1,0:T(8,128)S(1)}, f32[1,64,1024]{2,1,0:T(8,128)S(1)}, u32[]{:S(2)}, u32[]{:S(2)}) collective-permute-start(f32[1,64,1024]{2,1,0:T(8,128)S(1)} %get-tuple-element.66), channel_id=1, source_target_pairs={{0,4},{4,8},{8,12},{12,16},{16,20},{20,24},{24,28},{28,32},{32,36}... | collective-permute-start | bytes 786440 | tf_op jit(solution)/shard_map/while/body/eval_jaxpr/ppermute | solution.py:107
  98.8 9.8 %collective-permute-start = (f32[1,64,1024]{2,1,0:T(8,128)S(1)}, f32[1,64,1024]{2,1,0:T(8,128)S(1)}, u32[]{:S(2)}, u32[]{:S(2)}) collective-permute-start(f32[1,64,1024]{2,1,0:T(8,128)S(1)} %get-tuple-element.66), channel_id=1, source_target_pairs={{0,4},{4,8},{8,12},{12,16},{16,20},{20,24},{24,28},{28,32},{32,36}... | collective-permute-start | bytes 786440 | tf_op jit(solution)/shard_map/while/body/eval_jaxpr/ppermute | solution.py:107
  108.9 9.8 %collective-permute-start = (f32[1,64,1024]{2,1,0:T(8,128)S(1)}, f32[1,64,1024]{2,1,0:T(8,128)S(1)}, u32[]{:S(2)}, u32[]{:S(2)}) collective-permute-start(f32[1,64,1024]{2,1,0:T(8,128)S(1)} %get-tuple-element.66), channel_id=1, source_target_pairs={{0,4},{4,8},{8,12},{12,16},{16,20},{20,24},{24,28},{28,32},{32,36}... | collective-permute-start | bytes 786440 | tf_op jit(solution)/shard_map/while/body/eval_jaxpr/ppermute | solution.py:107
  119.1 9.8 %collective-permute-start = (f32[1,64,1024]{2,1,0:T(8,128)S(1)}, f32[1,64,1024]{2,1,0:T(8,128)S(1)}, u32[]{:S(2)}, u32[]{:S(2)}) collective-permute-start(f32[1,64,1024]{2,1,0:T(8,128)S(1)} %get-tuple-element.66), channel_id=1, source_target_pairs={{0,4},{4,8},{8,12},{12,16},{16,20},{20,24},{24,28},{28,32},{32,36}... | collective-permute-start | bytes 786440 | tf_op jit(solution)/shard_map/while/body/eval_jaxpr/ppermute | solution.py:107
  129.3 9.8 %collective-permute-start = (f32[1,64,1024]{2,1,0:T(8,128)S(1)}, f32[1,64,1024]{2,1,0:T(8,128)S(1)}, u32[]{:S(2)}, u32[]{:S(2)}) collective-permute-start(f32[1,64,1024]{2,1,0:T(8,128)S(1)} %get-tuple-element.66), channel_id=1, source_target_pairs={{0,4},{4,8},{8,12},{12,16},{16,20},{20,24},{24,28},{28,32},{32,36}... | collective-permute-start | bytes 786440 | tf_op jit(solution)/shard_map/while/body/eval_jaxpr/ppermute | solution.py:107
  139.5 9.8 %collective-permute-start = (f32[1,64,1024]{2,1,0:T(8,128)S(1)}, f32[1,64,1024]{2,1,0:T(8,128)S(1)}, u32[]{:S(2)}, u32[]{:S(2)}) collective-permute-start(f32[1,64,1024]{2,1,0:T(8,128)S(1)} %get-tuple-element.66), channel_id=1, source_target_pairs={{0,4},{4,8},{8,12},{12,16},{16,20},{20,24},{24,28},{28,32},{32,36}... | collective-permute-start | bytes 786440 | tf_op jit(solution)/shard_map/while/body/eval_jaxpr/ppermute | solution.py:107
  149.7 9.8 %collective-permute-start = (f32[1,64,1024]{2,1,0:T(8,128)S(1)}, f32[1,64,1024]{2,1,0:T(8,128)S(1)}, u32[]{:S(2)}, u32[]{:S(2)}) collective-permute-start(f32[1,64,1024]{2,1,0:T(8,128)S(1)} %get-tuple-element.66), channel_id=1, source_target_pairs={{0,4},{4,8},{8,12},{12,16},{16,20},{20,24},{24,28},{28,32},{32,36}... | collective-permute-start | bytes 786440 | tf_op jit(solution)/shard_map/while/body/eval_jaxpr/ppermute | solution.py:107
  159.9 9.8 %collective-permute-start = (f32[1,64,1024]{2,1,0:T(8,128)S(1)}, f32[1,64,1024]{2,1,0:T(8,128)S(1)}, u32[]{:S(2)}, u32[]{:S(2)}) collective-permute-start(f32[1,64,1024]{2,1,0:T(8,128)S(1)} %get-tuple-element.66), channel_id=1, source_target_pairs={{0,4},{4,8},{8,12},{12,16},{16,20},{20,24},{24,28},{28,32},{32,36}... | collective-permute-start | bytes 786440 | tf_op jit(solution)/shard_map/while/body/eval_jaxpr/ppermute | solution.py:107
  170.1 9.8 %collective-permute-start = (f32[1,64,1024]{2,1,0:T(8,128)S(1)}, f32[1,64,1024]{2,1,0:T(8,128)S(1)}, u32[]{:S(2)}, u32[]{:S(2)}) collective-permute-start(f32[1,64,1024]{2,1,0:T(8,128)S(1)} %get-tuple-element.66), channel_id=1, source_target_pairs={{0,4},{4,8},{8,12},{12,16},{16,20},{20,24},{24,28},{28,32},{32,36}... | collective-permute-start | bytes 786440 | tf_op jit(solution)/shard_map/while/body/eval_jaxpr/ppermute | solution.py:107
  180.3 9.8 %collective-permute-start = (f32[1,64,1024]{2,1,0:T(8,128)S(1)}, f32[1,64,1024]{2,1,0:T(8,128)S(1)}, u32[]{:S(2)}, u32[]{:S(2)}) collective-permute-start(f32[1,64,1024]{2,1,0:T(8,128)S(1)} %get-tuple-element.66), channel_id=1, source_target_pairs={{0,4},{4,8},{8,12},{12,16},{16,20},{20,24},{24,28},{28,32},{32,36}... | collective-permute-start | bytes 786440 | tf_op jit(solution)/shard_map/while/body/eval_jaxpr/ppermute | solution.py:107
  190.5 9.8 %collective-permute-start = (f32[1,64,1024]{2,1,0:T(8,128)S(1)}, f32[1,64,1024]{2,1,0:T(8,128)S(1)}, u32[]{:S(2)}, u32[]{:S(2)}) collective-permute-start(f32[1,64,1024]{2,1,0:T(8,128)S(1)} %get-tuple-element.66), channel_id=1, source_target_pairs={{0,4},{4,8},{8,12},{12,16},{16,20},{20,24},{24,28},{28,32},{32,36}... | collective-permute-start | bytes 786440 | tf_op jit(solution)/shard_map/while/body/eval_jaxpr/ppermute | solution.py:107
  200.7 9.8 %collective-permute-start = (f32[1,64,1024]{2,1,0:T(8,128)S(1)}, f32[1,64,1024]{2,1,0:T(8,128)S(1)}, u32[]{:S(2)}, u32[]{:S(2)}) collective-permute-start(f32[1,64,1024]{2,1,0:T(8,128)S(1)} %get-tuple-element.66), channel_id=1, source_target_pairs={{0,4},{4,8},{8,12},{12,16},{16,20},{20,24},{24,28},{28,32},{32,36}... | collective-permute-start | bytes 786440 | tf_op jit(solution)/shard_map/while/body/eval_jaxpr/ppermute | solution.py:107
  210.8 9.8 %collective-permute-start = (f32[1,64,1024]{2,1,0:T(8,128)S(1)}, f32[1,64,1024]{2,1,0:T(8,128)S(1)}, u32[]{:S(2)}, u32[]{:S(2)}) collective-permute-start(f32[1,64,1024]{2,1,0:T(8,128)S(1)} %get-tuple-element.66), channel_id=1, source_target_pairs={{0,4},{4,8},{8,12},{12,16},{16,20},{20,24},{24,28},{28,32},{32,36}... | collective-permute-start | bytes 786440 | tf_op jit(solution)/shard_map/while/body/eval_jaxpr/ppermute | solution.py:107
  221.0 9.8 %collective-permute-start = (f32[1,64,1024]{2,1,0:T(8,128)S(1)}, f32[1,64,1024]{2,1,0:T(8,128)S(1)}, u32[]{:S(2)}, u32[]{:S(2)}) collective-permute-start(f32[1,64,1024]{2,1,0:T(8,128)S(1)} %get-tuple-element.66), channel_id=1, source_target_pairs={{0,4},{4,8},{8,12},{12,16},{16,20},{20,24},{24,28},{28,32},{32,36}... | collective-permute-start | bytes 786440 | tf_op jit(solution)/shard_map/while/body/eval_jaxpr/ppermute | solution.py:107
  231.2 9.8 %collective-permute-start = (f32[1,64,1024]{2,1,0:T(8,128)S(1)}, f32[1,64,1024]{2,1,0:T(8,128)S(1)}, u32[]{:S(2)}, u32[]{:S(2)}) collective-permute-start(f32[1,64,1024]{2,1,0:T(8,128)S(1)} %get-tuple-element.66), channel_id=1, source_target_pairs={{0,4},{4,8},{8,12},{12,16},{16,20},{20,24},{24,28},{28,32},{32,36}... | collective-permute-start | bytes 786440 | tf_op jit(solution)/shard_map/while/body/eval_jaxpr/ppermute | solution.py:107
  241.4 9.8 %collective-permute-start = (f32[1,64,1024]{2,1,0:T(8,128)S(1)}, f32[1,64,1024]{2,1,0:T(8,128)S(1)}, u32[]{:S(2)}, u32[]{:S(2)}) collective-permute-start(f32[1,64,1024]{2,1,0:T(8,128)S(1)} %get-tuple-element.66), channel_id=1, source_target_pairs={{0,4},{4,8},{8,12},{12,16},{16,20},{20,24},{24,28},{28,32},{32,36}... | collective-permute-start | bytes 786440 | tf_op jit(solution)/shard_map/while/body/eval_jaxpr/ppermute | solution.py:107
  251.6 9.8 %collective-permute-start = (f32[1,64,1024]{2,1,0:T(8,128)S(1)}, f32[1,64,1024]{2,1,0:T(8,128)S(1)}, u32[]{:S(2)}, u32[]{:S(2)}) collective-permute-start(f32[1,64,1024]{2,1,0:T(8,128)S(1)} %get-tuple-element.66), channel_id=1, source_target_pairs={{0,4},{4,8},{8,12},{12,16},{16,20},{20,24},{24,28},{28,32},{32,36}... | collective-permute-start | bytes 786440 | tf_op jit(solution)/shard_map/while/body/eval_jaxpr/ppermute | solution.py:107
  261.8 9.8 %collective-permute-start = (f32[1,64,1024]{2,1,0:T(8,128)S(1)}, f32[1,64,1024]{2,1,0:T(8,128)S(1)}, u32[]{:S(2)}, u32[]{:S(2)}) collective-permute-start(f32[1,64,1024]{2,1,0:T(8,128)S(1)} %get-tuple-element.66), channel_id=1, source_target_pairs={{0,4},{4,8},{8,12},{12,16},{16,20},{20,24},{24,28},{28,32},{32,36}... | collective-permute-start | bytes 786440 | tf_op jit(solution)/shard_map/while/body/eval_jaxpr/ppermute | solution.py:107
  272.0 9.8 %collective-permute-start = (f32[1,64,1024]{2,1,0:T(8,128)S(1)}, f32[1,64,1024]{2,1,0:T(8,128)S(1)}, u32[]{:S(2)}, u32[]{:S(2)}) collective-permute-start(f32[1,64,1024]{2,1,0:T(8,128)S(1)} %get-tuple-element.66), channel_id=1, source_target_pairs={{0,4},{4,8},{8,12},{12,16},{16,20},{20,24},{24,28},{28,32},{32,36}... | collective-permute-start | bytes 786440 | tf_op jit(solution)/shard_map/while/body/eval_jaxpr/ppermute | solution.py:107
  282.2 9.8 %collective-permute-start = (f32[1,64,1024]{2,1,0:T(8,128)S(1)}, f32[1,64,1024]{2,1,0:T(8,128)S(1)}, u32[]{:S(2)}, u32[]{:S(2)}) collective-permute-start(f32[1,64,1024]{2,1,0:T(8,128)S(1)} %get-tuple-element.66), channel_id=1, source_target_pairs={{0,4},{4,8},{8,12},{12,16},{16,20},{20,24},{24,28},{28,32},{32,36}... | collective-permute-start | bytes 786440 | tf_op jit(solution)/shard_map/while/body/eval_jaxpr/ppermute | solution.py:107
  292.4 9.8 %collective-permute-start = (f32[1,64,1024]{2,1,0:T(8,128)S(1)}, f32[1,64,1024]{2,1,0:T(8,128)S(1)}, u32[]{:S(2)}, u32[]{:S(2)}) collective-permute-start(f32[1,64,1024]{2,1,0:T(8,128)S(1)} %get-tuple-element.66), channel_id=1, source_target_pairs={{0,4},{4,8},{8,12},{12,16},{16,20},{20,24},{24,28},{28,32},{32,36}... | collective-permute-start | bytes 786440 | tf_op jit(solution)/shard_map/while/body/eval_jaxpr/ppermute | solution.py:107
  302.5 9.8 %collective-permute-start = (f32[1,64,1024]{2,1,0:T(8,128)S(1)}, f32[1,64,1024]{2,1,0:T(8,128)S(1)}, u32[]{:S(2)}, u32[]{:S(2)}) collective-permute-start(f32[1,64,1024]{2,1,0:T(8,128)S(1)} %get-tuple-element.66), channel_id=1, source_target_pairs={{0,4},{4,8},{8,12},{12,16},{16,20},{20,24},{24,28},{28,32},{32,36}... | collective-permute-start | bytes 786440 | tf_op jit(solution)/shard_map/while/body/eval_jaxpr/ppermute | solution.py:107
  312.7 9.8 %collective-permute-start = (f32[1,64,1024]{2,1,0:T(8,128)S(1)}, f32[1,64,1024]{2,1,0:T(8,128)S(1)}, u32[]{:S(2)}, u32[]{:S(2)}) collective-permute-start(f32[1,64,1024]{2,1,0:T(8,128)S(1)} %get-tuple-element.66), channel_id=1, source_target_pairs={{0,4},{4,8},{8,12},{12,16},{16,20},{20,24},{24,28},{28,32},{32,36}... | collective-permute-start | bytes 786440 | tf_op jit(solution)/shard_map/while/body/eval_jaxpr/ppermute | solution.py:107
  322.9 9.8 %collective-permute-start = (f32[1,64,1024]{2,1,0:T(8,128)S(1)}, f32[1,64,1024]{2,1,0:T(8,128)S(1)}, u32[]{:S(2)}, u32[]{:S(2)}) collective-permute-start(f32[1,64,1024]{2,1,0:T(8,128)S(1)} %get-tuple-element.66), channel_id=1, source_target_pairs={{0,4},{4,8},{8,12},{12,16},{16,20},{20,24},{24,28},{28,32},{32,36}... | collective-permute-start | bytes 786440 | tf_op jit(solution)/shard_map/while/body/eval_jaxpr/ppermute | solution.py:107
  333.1 9.8 %collective-permute-start = (f32[1,64,1024]{2,1,0:T(8,128)S(1)}, f32[1,64,1024]{2,1,0:T(8,128)S(1)}, u32[]{:S(2)}, u32[]{:S(2)}) collective-permute-start(f32[1,64,1024]{2,1,0:T(8,128)S(1)} %get-tuple-element.66), channel_id=1, source_target_pairs={{0,4},{4,8},{8,12},{12,16},{16,20},{20,24},{24,28},{28,32},{32,36}... | collective-permute-start | bytes 786440 | tf_op jit(solution)/shard_map/while/body/eval_jaxpr/ppermute | solution.py:107
  343.3 9.8 %collective-permute-start = (f32[1,64,1024]{2,1,0:T(8,128)S(1)}, f32[1,64,1024]{2,1,0:T(8,128)S(1)}, u32[]{:S(2)}, u32[]{:S(2)}) collective-permute-start(f32[1,64,1024]{2,1,0:T(8,128)S(1)} %get-tuple-element.66), channel_id=1, source_target_pairs={{0,4},{4,8},{8,12},{12,16},{16,20},{20,24},{24,28},{28,32},{32,36}... | collective-permute-start | bytes 786440 | tf_op jit(solution)/shard_map/while/body/eval_jaxpr/ppermute | solution.py:107
  353.5 9.8 %collective-permute-start = (f32[1,64,1024]{2,1,0:T(8,128)S(1)}, f32[1,64,1024]{2,1,0:T(8,128)S(1)}, u32[]{:S(2)}, u32[]{:S(2)}) collective-permute-start(f32[1,64,1024]{2,1,0:T(8,128)S(1)} %get-tuple-element.66), channel_id=1, source_target_pairs={{0,4},{4,8},{8,12},{12,16},{16,20},{20,24},{24,28},{28,32},{32,36}... | collective-permute-start | bytes 786440 | tf_op jit(solution)/shard_map/while/body/eval_jaxpr/ppermute | solution.py:107
  363.7 9.8 %collective-permute-start = (f32[1,64,1024]{2,1,0:T(8,128)S(1)}, f32[1,64,1024]{2,1,0:T(8,128)S(1)}, u32[]{:S(2)}, u32[]{:S(2)}) collective-permute-start(f32[1,64,1024]{2,1,0:T(8,128)S(1)} %get-tuple-element.66), channel_id=1, source_target_pairs={{0,4},{4,8},{8,12},{12,16},{16,20},{20,24},{24,28},{28,32},{32,36}... | collective-permute-start | bytes 786440 | tf_op jit(solution)/shard_map/while/body/eval_jaxpr/ppermute | solution.py:107
  373.9 9.8 %collective-permute-start = (f32[1,64,1024]{2,1,0:T(8,128)S(1)}, f32[1,64,1024]{2,1,0:T(8,128)S(1)}, u32[]{:S(2)}, u32[]{:S(2)}) collective-permute-start(f32[1,64,1024]{2,1,0:T(8,128)S(1)} %get-tuple-element.66), channel_id=1, source_target_pairs={{0,4},{4,8},{8,12},{12,16},{16,20},{20,24},{24,28},{28,32},{32,36}... | collective-permute-start | bytes 786440 | tf_op jit(solution)/shard_map/while/body/eval_jaxpr/ppermute | solution.py:107
  384.1 9.8 %collective-permute-start = (f32[1,64,1024]{2,1,0:T(8,128)S(1)}, f32[1,64,1024]{2,1,0:T(8,128)S(1)}, u32[]{:S(2)}, u32[]{:S(2)}) collective-permute-start(f32[1,64,1024]{2,1,0:T(8,128)S(1)} %get-tuple-element.66), channel_id=1, source_target_pairs={{0,4},{4,8},{8,12},{12,16},{16,20},{20,24},{24,28},{28,32},{32,36}... | collective-permute-start | bytes 786440 | tf_op jit(solution)/shard_map/while/body/eval_jaxpr/ppermute | solution.py:107
  394.3 9.8 %collective-permute-start = (f32[1,64,1024]{2,1,0:T(8,128)S(1)}, f32[1,64,1024]{2,1,0:T(8,128)S(1)}, u32[]{:S(2)}, u32[]{:S(2)}) collective-permute-start(f32[1,64,1024]{2,1,0:T(8,128)S(1)} %get-tuple-element.66), channel_id=1, source_target_pairs={{0,4},{4,8},{8,12},{12,16},{16,20},{20,24},{24,28},{28,32},{32,36}... | collective-permute-start | bytes 786440 | tf_op jit(solution)/shard_map/while/body/eval_jaxpr/ppermute | solution.py:107
  404.4 9.8 %collective-permute-start = (f32[1,64,1024]{2,1,0:T(8,128)S(1)}, f32[1,64,1024]{2,1,0:T(8,128)S(1)}, u32[]{:S(2)}, u32[]{:S(2)}) collective-permute-start(f32[1,64,1024]{2,1,0:T(8,128)S(1)} %get-tuple-element.66), channel_id=1, source_target_pairs={{0,4},{4,8},{8,12},{12,16},{16,20},{20,24},{24,28},{28,32},{32,36}... | collective-permute-start | bytes 786440 | tf_op jit(solution)/shard_map/while/body/eval_jaxpr/ppermute | solution.py:107
  414.6 9.8 %collective-permute-start = (f32[1,64,1024]{2,1,0:T(8,128)S(1)}, f32[1,64,1024]{2,1,0:T(8,128)S(1)}, u32[]{:S(2)}, u32[]{:S(2)}) collective-permute-start(f32[1,64,1024]{2,1,0:T(8,128)S(1)} %get-tuple-element.66), channel_id=1, source_target_pairs={{0,4},{4,8},{8,12},{12,16},{16,20},{20,24},{24,28},{28,32},{32,36}... | collective-permute-start | bytes 786440 | tf_op jit(solution)/shard_map/while/body/eval_jaxpr/ppermute | solution.py:107
  424.8 9.8 %collective-permute-start = (f32[1,64,1024]{2,1,0:T(8,128)S(1)}, f32[1,64,1024]{2,1,0:T(8,128)S(1)}, u32[]{:S(2)}, u32[]{:S(2)}) collective-permute-start(f32[1,64,1024]{2,1,0:T(8,128)S(1)} %get-tuple-element.66), channel_id=1, source_target_pairs={{0,4},{4,8},{8,12},{12,16},{16,20},{20,24},{24,28},{28,32},{32,36}... | collective-permute-start | bytes 786440 | tf_op jit(solution)/shard_map/while/body/eval_jaxpr/ppermute | solution.py:107
  435.0 9.8 %collective-permute-start = (f32[1,64,1024]{2,1,0:T(8,128)S(1)}, f32[1,64,1024]{2,1,0:T(8,128)S(1)}, u32[]{:S(2)}, u32[]{:S(2)}) collective-permute-start(f32[1,64,1024]{2,1,0:T(8,128)S(1)} %get-tuple-element.66), channel_id=1, source_target_pairs={{0,4},{4,8},{8,12},{12,16},{16,20},{20,24},{24,28},{28,32},{32,36}... | collective-permute-start | bytes 786440 | tf_op jit(solution)/shard_map/while/body/eval_jaxpr/ppermute | solution.py:107
  445.2 9.8 %collective-permute-start = (f32[1,64,1024]{2,1,0:T(8,128)S(1)}, f32[1,64,1024]{2,1,0:T(8,128)S(1)}, u32[]{:S(2)}, u32[]{:S(2)}) collective-permute-start(f32[1,64,1024]{2,1,0:T(8,128)S(1)} %get-tuple-element.66), channel_id=1, source_target_pairs={{0,4},{4,8},{8,12},{12,16},{16,20},{20,24},{24,28},{28,32},{32,36}... | collective-permute-start | bytes 786440 | tf_op jit(solution)/shard_map/while/body/eval_jaxpr/ppermute | solution.py:107
  455.4 9.8 %collective-permute-start = (f32[1,64,1024]{2,1,0:T(8,128)S(1)}, f32[1,64,1024]{2,1,0:T(8,128)S(1)}, u32[]{:S(2)}, u32[]{:S(2)}) collective-permute-start(f32[1,64,1024]{2,1,0:T(8,128)S(1)} %get-tuple-element.66), channel_id=1, source_target_pairs={{0,4},{4,8},{8,12},{12,16},{16,20},{20,24},{24,28},{28,32},{32,36}... | collective-permute-start | bytes 786440 | tf_op jit(solution)/shard_map/while/body/eval_jaxpr/ppermute | solution.py:107
  465.6 9.8 %collective-permute-start = (f32[1,64,1024]{2,1,0:T(8,128)S(1)}, f32[1,64,1024]{2,1,0:T(8,128)S(1)}, u32[]{:S(2)}, u32[]{:S(2)}) collective-permute-start(f32[1,64,1024]{2,1,0:T(8,128)S(1)} %get-tuple-element.66), channel_id=1, source_target_pairs={{0,4},{4,8},{8,12},{12,16},{16,20},{20,24},{24,28},{28,32},{32,36}... | collective-permute-start | bytes 786440 | tf_op jit(solution)/shard_map/while/body/eval_jaxpr/ppermute | solution.py:107
  475.8 9.8 %collective-permute-start = (f32[1,64,1024]{2,1,0:T(8,128)S(1)}, f32[1,64,1024]{2,1,0:T(8,128)S(1)}, u32[]{:S(2)}, u32[]{:S(2)}) collective-permute-start(f32[1,64,1024]{2,1,0:T(8,128)S(1)} %get-tuple-element.66), channel_id=1, source_target_pairs={{0,4},{4,8},{8,12},{12,16},{16,20},{20,24},{24,28},{28,32},{32,36}... | collective-permute-start | bytes 786440 | tf_op jit(solution)/shard_map/while/body/eval_jaxpr/ppermute | solution.py:107
  486.0 9.8 %collective-permute-start = (f32[1,64,1024]{2,1,0:T(8,128)S(1)}, f32[1,64,1024]{2,1,0:T(8,128)S(1)}, u32[]{:S(2)}, u32[]{:S(2)}) collective-permute-start(f32[1,64,1024]{2,1,0:T(8,128)S(1)} %get-tuple-element.66), channel_id=1, source_target_pairs={{0,4},{4,8},{8,12},{12,16},{16,20},{20,24},{24,28},{28,32},{32,36}... | collective-permute-start | bytes 786440 | tf_op jit(solution)/shard_map/while/body/eval_jaxpr/ppermute | solution.py:107
  496.1 9.8 %collective-permute-start = (f32[1,64,1024]{2,1,0:T(8,128)S(1)}, f32[1,64,1024]{2,1,0:T(8,128)S(1)}, u32[]{:S(2)}, u32[]{:S(2)}) collective-permute-start(f32[1,64,1024]{2,1,0:T(8,128)S(1)} %get-tuple-element.66), channel_id=1, source_target_pairs={{0,4},{4,8},{8,12},{12,16},{16,20},{20,24},{24,28},{28,32},{32,36}... | collective-permute-start | bytes 786440 | tf_op jit(solution)/shard_map/while/body/eval_jaxpr/ppermute | solution.py:107
  506.3 9.8 %collective-permute-start = (f32[1,64,1024]{2,1,0:T(8,128)S(1)}, f32[1,64,1024]{2,1,0:T(8,128)S(1)}, u32[]{:S(2)}, u32[]{:S(2)}) collective-permute-start(f32[1,64,1024]{2,1,0:T(8,128)S(1)} %get-tuple-element.66), channel_id=1, source_target_pairs={{0,4},{4,8},{8,12},{12,16},{16,20},{20,24},{24,28},{28,32},{32,36}... | collective-permute-start | bytes 786440 | tf_op jit(solution)/shard_map/while/body/eval_jaxpr/ppermute | solution.py:107
  516.5 9.8 %collective-permute-start = (f32[1,64,1024]{2,1,0:T(8,128)S(1)}, f32[1,64,1024]{2,1,0:T(8,128)S(1)}, u32[]{:S(2)}, u32[]{:S(2)}) collective-permute-start(f32[1,64,1024]{2,1,0:T(8,128)S(1)} %get-tuple-element.66), channel_id=1, source_target_pairs={{0,4},{4,8},{8,12},{12,16},{16,20},{20,24},{24,28},{28,32},{32,36}... | collective-permute-start | bytes 786440 | tf_op jit(solution)/shard_map/while/body/eval_jaxpr/ppermute | solution.py:107
  526.7 9.8 %collective-permute-start = (f32[1,64,1024]{2,1,0:T(8,128)S(1)}, f32[1,64,1024]{2,1,0:T(8,128)S(1)}, u32[]{:S(2)}, u32[]{:S(2)}) collective-permute-start(f32[1,64,1024]{2,1,0:T(8,128)S(1)} %get-tuple-element.66), channel_id=1, source_target_pairs={{0,4},{4,8},{8,12},{12,16},{16,20},{20,24},{24,28},{28,32},{32,36}... | collective-permute-start | bytes 786440 | tf_op jit(solution)/shard_map/while/body/eval_jaxpr/ppermute | solution.py:107
  536.9 9.8 %collective-permute-start = (f32[1,64,1024]{2,1,0:T(8,128)S(1)}, f32[1,64,1024]{2,1,0:T(8,128)S(1)}, u32[]{:S(2)}, u32[]{:S(2)}) collective-permute-start(f32[1,64,1024]{2,1,0:T(8,128)S(1)} %get-tuple-element.66), channel_id=1, source_target_pairs={{0,4},{4,8},{8,12},{12,16},{16,20},{20,24},{24,28},{28,32},{32,36}... | collective-permute-start | bytes 786440 | tf_op jit(solution)/shard_map/while/body/eval_jaxpr/ppermute | solution.py:107
  547.1 9.8 %collective-permute-start = (f32[1,64,1024]{2,1,0:T(8,128)S(1)}, f32[1,64,1024]{2,1,0:T(8,128)S(1)}, u32[]{:S(2)}, u32[]{:S(2)}) collective-permute-start(f32[1,64,1024]{2,1,0:T(8,128)S(1)} %get-tuple-element.66), channel_id=1, source_target_pairs={{0,4},{4,8},{8,12},{12,16},{16,20},{20,24},{24,28},{28,32},{32,36}... | collective-permute-start | bytes 786440 | tf_op jit(solution)/shard_map/while/body/eval_jaxpr/ppermute | solution.py:107
  557.3 9.8 %collective-permute-start = (f32[1,64,1024]{2,1,0:T(8,128)S(1)}, f32[1,64,1024]{2,1,0:T(8,128)S(1)}, u32[]{:S(2)}, u32[]{:S(2)}) collective-permute-start(f32[1,64,1024]{2,1,0:T(8,128)S(1)} %get-tuple-element.66), channel_id=1, source_target_pairs={{0,4},{4,8},{8,12},{12,16},{16,20},{20,24},{24,28},{28,32},{32,36}... | collective-permute-start | bytes 786440 | tf_op jit(solution)/shard_map/while/body/eval_jaxpr/ppermute | solution.py:107
  567.5 9.8 %collective-permute-start = (f32[1,64,1024]{2,1,0:T(8,128)S(1)}, f32[1,64,1024]{2,1,0:T(8,128)S(1)}, u32[]{:S(2)}, u32[]{:S(2)}) collective-permute-start(f32[1,64,1024]{2,1,0:T(8,128)S(1)} %get-tuple-element.66), channel_id=1, source_target_pairs={{0,4},{4,8},{8,12},{12,16},{16,20},{20,24},{24,28},{28,32},{32,36}... | collective-permute-start | bytes 786440 | tf_op jit(solution)/shard_map/while/body/eval_jaxpr/ppermute | solution.py:107
  577.7 9.8 %collective-permute-start = (f32[1,64,1024]{2,1,0:T(8,128)S(1)}, f32[1,64,1024]{2,1,0:T(8,128)S(1)}, u32[]{:S(2)}, u32[]{:S(2)}) collective-permute-start(f32[1,64,1024]{2,1,0:T(8,128)S(1)} %get-tuple-element.66), channel_id=1, source_target_pairs={{0,4},{4,8},{8,12},{12,16},{16,20},{20,24},{24,28},{28,32},{32,36}... | collective-permute-start | bytes 786440 | tf_op jit(solution)/shard_map/while/body/eval_jaxpr/ppermute | solution.py:107
  587.9 9.8 %collective-permute-start = (f32[1,64,1024]{2,1,0:T(8,128)S(1)}, f32[1,64,1024]{2,1,0:T(8,128)S(1)}, u32[]{:S(2)}, u32[]{:S(2)}) collective-permute-start(f32[1,64,1024]{2,1,0:T(8,128)S(1)} %get-tuple-element.66), channel_id=1, source_target_pairs={{0,4},{4,8},{8,12},{12,16},{16,20},{20,24},{24,28},{28,32},{32,36}... | collective-permute-start | bytes 786440 | tf_op jit(solution)/shard_map/while/body/eval_jaxpr/ppermute | solution.py:107
  598.0 9.8 %collective-permute-start = (f32[1,64,1024]{2,1,0:T(8,128)S(1)}, f32[1,64,1024]{2,1,0:T(8,128)S(1)}, u32[]{:S(2)}, u32[]{:S(2)}) collective-permute-start(f32[1,64,1024]{2,1,0:T(8,128)S(1)} %get-tuple-element.66), channel_id=1, source_target_pairs={{0,4},{4,8},{8,12},{12,16},{16,20},{20,24},{24,28},{28,32},{32,36}... | collective-permute-start | bytes 786440 | tf_op jit(solution)/shard_map/while/body/eval_jaxpr/ppermute | solution.py:107
  608.2 9.8 %collective-permute-start = (f32[1,64,1024]{2,1,0:T(8,128)S(1)}, f32[1,64,1024]{2,1,0:T(8,128)S(1)}, u32[]{:S(2)}, u32[]{:S(2)}) collective-permute-start(f32[1,64,1024]{2,1,0:T(8,128)S(1)} %get-tuple-element.66), channel_id=1, source_target_pairs={{0,4},{4,8},{8,12},{12,16},{16,20},{20,24},{24,28},{28,32},{32,36}... | collective-permute-start | bytes 786440 | tf_op jit(solution)/shard_map/while/body/eval_jaxpr/ppermute | solution.py:107
  618.4 9.8 %collective-permute-start = (f32[1,64,1024]{2,1,0:T(8,128)S(1)}, f32[1,64,1024]{2,1,0:T(8,128)S(1)}, u32[]{:S(2)}, u32[]{:S(2)}) collective-permute-start(f32[1,64,1024]{2,1,0:T(8,128)S(1)} %get-tuple-element.66), channel_id=1, source_target_pairs={{0,4},{4,8},{8,12},{12,16},{16,20},{20,24},{24,28},{28,32},{32,36}... | collective-permute-start | bytes 786440 | tf_op jit(solution)/shard_map/while/body/eval_jaxpr/ppermute | solution.py:107
  628.6 9.8 %collective-permute-start = (f32[1,64,1024]{2,1,0:T(8,128)S(1)}, f32[1,64,1024]{2,1,0:T(8,128)S(1)}, u32[]{:S(2)}, u32[]{:S(2)}) collective-permute-start(f32[1,64,1024]{2,1,0:T(8,128)S(1)} %get-tuple-element.66), channel_id=1, source_target_pairs={{0,4},{4,8},{8,12},{12,16},{16,20},{20,24},{24,28},{28,32},{32,36}... | collective-permute-start | bytes 786440 | tf_op jit(solution)/shard_map/while/body/eval_jaxpr/ppermute | solution.py:107
  638.8 9.8 %collective-permute-start = (f32[1,64,1024]{2,1,0:T(8,128)S(1)}, f32[1,64,1024]{2,1,0:T(8,128)S(1)}, u32[]{:S(2)}, u32[]{:S(2)}) collective-permute-start(f32[1,64,1024]{2,1,0:T(8,128)S(1)} %get-tuple-element.66), channel_id=1, source_target_pairs={{0,4},{4,8},{8,12},{12,16},{16,20},{20,24},{24,28},{28,32},{32,36}... | collective-permute-start | bytes 786440 | tf_op jit(solution)/shard_map/while/body/eval_jaxpr/ppermute | solution.py:107
  649.0 9.8 %collective-permute-start = (f32[1,64,1024]{2,1,0:T(8,128)S(1)}, f32[1,64,1024]{2,1,0:T(8,128)S(1)}, u32[]{:S(2)}, u32[]{:S(2)}) collective-permute-start(f32[1,64,1024]{2,1,0:T(8,128)S(1)} %get-tuple-element.66), channel_id=1, source_target_pairs={{0,4},{4,8},{8,12},{12,16},{16,20},{20,24},{24,28},{28,32},{32,36}... | collective-permute-start | bytes 786440 | tf_op jit(solution)/shard_map/while/body/eval_jaxpr/ppermute | solution.py:107
  659.2 9.8 %collective-permute-start = (f32[1,64,1024]{2,1,0:T(8,128)S(1)}, f32[1,64,1024]{2,1,0:T(8,128)S(1)}, u32[]{:S(2)}, u32[]{:S(2)}) collective-permute-start(f32[1,64,1024]{2,1,0:T(8,128)S(1)} %get-tuple-element.66), channel_id=1, source_target_pairs={{0,4},{4,8},{8,12},{12,16},{16,20},{20,24},{24,28},{28,32},{32,36}... | collective-permute-start | bytes 786440 | tf_op jit(solution)/shard_map/while/body/eval_jaxpr/ppermute | solution.py:107
  669.4 9.8 %collective-permute-start = (f32[1,64,1024]{2,1,0:T(8,128)S(1)}, f32[1,64,1024]{2,1,0:T(8,128)S(1)}, u32[]{:S(2)}, u32[]{:S(2)}) collective-permute-start(f32[1,64,1024]{2,1,0:T(8,128)S(1)} %get-tuple-element.66), channel_id=1, source_target_pairs={{0,4},{4,8},{8,12},{12,16},{16,20},{20,24},{24,28},{28,32},{32,36}... | collective-permute-start | bytes 786440 | tf_op jit(solution)/shard_map/while/body/eval_jaxpr/ppermute | solution.py:107
  (4 other events, 109.9 us)

commit v2 on v1

--- a/solution.py
+++ b/solution.py
@@ -43,7 +43,7 @@
     return [value[:, LANES * k : LANES * (k + 1)] for k in range(value.shape[1] // LANES)]
 
 
-def conv_layers(state_ref, weight_ref, bias_ref, unroll):
+def conv_layers(state_ref, weight_ref, bias_ref, first, last, unroll=1):
     ch = state_ref.shape[1]
     lane = lax.broadcasted_iota(jnp.int32, (ch, LANES), 1)
     column = lane % SIDE
@@ -78,55 +78,173 @@
             state_ref[band] = state_ref[band] + step_size * jnp.tanh(mixed + bias)
         return unused
 
-    lax.fori_loop(0, weight_ref.shape[0], layer, 0, unroll=unroll)
-
-
-def block_kernel(start_ref, weight_ref, bias_ref, final_ref, state, unroll=1):
+    lax.fori_loop(first, last, layer, 0, unroll=unroll)
+
+
+def split_float(value):
+    coarse = value.astype(jnp.bfloat16)
+    return coarse, (value - coarse.astype(jnp.float32)).astype(jnp.bfloat16)
+
+
+def cycle_kernel(
+    count,
+    start_ref,
+    input_ref,
+    weight_ref,
+    bias_ref,
+    matrix_ref,
+    final_ref,
+    corrected_ref,
+    state,
+    origin,
+    matrix_t,
+    start_t,
+    ends_t,
+    input_t,
+    matrices,
+    starts,
+    ends,
+    chain,
+    returned,
+    send_sems,
+    recv_sems,
+):
+    me = lax.axis_index("layer")
+    ch, pixels = start_ref.shape
+    layers = weight_ref.shape[0]
+    share = pixels // count
+    early = layers // 4
+
+    def slice_of(owner):
+        return pl.ds(pl.multiple_of(owner * share, share), share)
+
+    def push(source, target, number, peer):
+        return pltpu.make_async_remote_copy(
+            src_ref=source,
+            dst_ref=target,
+            send_sem=send_sems.at[number],
+            recv_sem=recv_sems.at[number],
+            device_id={"layer": peer},
+            device_id_type=pl.DeviceIdType.MESH,
+        )
+
+    def peers(action):
+        def turn(offset, unused):
+            action(lax.rem(me + offset, count))
+            return unused
+
+        lax.fori_loop(1, count, turn, 0)
+
+    def all_of(buffer, number):
+        part = buffer.at[pl.ds(0, count - 1)]
+        return push(part, part, number, lax.rem(me + 1, count))
+
+    barrier = pltpu.get_barrier_semaphore()
+    peers(
+        lambda peer: pl.semaphore_signal(
+            barrier, inc=1, device_id={"layer": peer}, device_id_type=pl.DeviceIdType.MESH
+        )
+    )
+    matrix_t[...] = matrix_ref[...].T
+    matrices[me] = matrix_ref[...].T
     for band, value in enumerate(to_bands(split_lanes(start_ref[...]))):
         state[band] = value
-    conv_layers(state, weight_ref, bias_ref, unroll)
+        origin[band] = value
+        start_t[LANES * band : LANES * (band + 1), :] = value.T
+    for band, value in enumerate(to_bands(split_lanes(input_ref[...]))):
+        input_t[LANES * band : LANES * (band + 1), :] = value.T
+    starts[me] = start_t[slice_of(me), :]
+    conv_layers(state, weight_ref, bias_ref, 0, early)
+
+    pl.semaphore_wait(barrier, count - 1)
+
+    def send_early(peer):
+        push(matrix_t, matrices.at[me], 0, peer).start()
+        push(start_t.at[slice_of(peer)], starts.at[me], 1, peer).start()
+
+    peers(send_early)
+    conv_layers(state, weight_ref, bias_ref, early, layers)
+
+    for band in range(8):
+        ends_t[LANES * band : LANES * (band + 1), :] = state[band].T
+    ends[me] = ends_t[slice_of(me), :]
+    peers(lambda peer: push(ends_t.at[slice_of(peer)], ends.at[me], 2, peer).start())
+    all_of(matrices, 0).wait_recv()
+    all_of(starts, 1).wait_recv()
+    all_of(ends, 2).wait_recv()
+
+    def give(index):
+        @pl.when(index != me)
+        def _():
+            push(chain.at[index], returned.at[me], 3, index).start()
+
+    def chain_step(index, current):
+        matrix_high, matrix_low = split_float(matrices[index - 1])
+        high, low = split_float(current)
+        both = jnp.dot(
+            jnp.concatenate([high, low], axis=0), matrix_high, preferred_element_type=jnp.float32
+        )
+        rest = jnp.dot(high, matrix_low, preferred_element_type=jnp.float32)
+        current = both[:share] + both[share:] + rest + (ends[index - 1] - starts[index])
+        chain[index] = current
+        give(index - 1)
+        return current
+
+    first = input_t[slice_of(me), :] - starts[0]
+    chain[0] = first
+    lax.fori_loop(1, count, chain_step, first, unroll=3)
+    give(count - 1)
+    returned[me] = chain[me]
+    all_of(returned, 3).wait_recv()
+
+    corrected = []
+    gathered = returned[...].reshape(pixels, ch)
+    for band in range(8):
+        part = gathered[LANES * band : LANES * (band + 1)]
+        corrected.append(origin[band] + part.T)
+        state[band] = corrected[band]
+    for tile, value in enumerate(from_bands(corrected)):
+        corrected_ref[:, LANES * tile : LANES * (tile + 1)] = value
+    conv_layers(state, weight_ref, bias_ref, 0, layers)
     for tile, value in enumerate(from_bands([state[band] for band in range(8)])):
         final_ref[:, LANES * tile : LANES * (tile + 1)] = value
-
-
-def relax_block(start, conv_weight, bias_wide, unroll=1):
-    ch, pixels = start.shape
-    return pl.pallas_call(
-        functools.partial(block_kernel, unroll=unroll),
-        out_shape=jax.ShapeDtypeStruct((ch, pixels), jnp.float32),
-        in_specs=[pl.BlockSpec(memory_space=pltpu.VMEM)] * 3,
-        out_specs=pl.BlockSpec(memory_space=pltpu.VMEM),
-        scratch_shapes=[pltpu.VMEM((8, ch, LANES), jnp.float32)],
-        compiler_params=pltpu.CompilerParams(vmem_limit_bytes=60 << 20),
-    )(start, conv_weight, bias_wide)
-
-
-def from_behind(value, axis, steps):
-    count = lax.axis_size(axis)
-    initial, last = (max(0, -steps), min(count, count - steps))
-    return lax.ppermute(value, axis, [(source, source + steps) for source in range(initial, last)])
-
-
-def apply_matrix(matrix, field):
-    return jnp.einsum("cd,idp->icp", matrix, field, precision=lax.Precision.HIGHEST)
+    for number, buffer in enumerate((matrices, starts, ends, returned)):
+        all_of(buffer, number).wait_send()
 
 
 def on_device(cpoints, network_input, conv_weight, conv_bias, coarse_matrix):
-    start = cpoints[0]
+    ch, pixels = network_input.shape[1:]
+    count = lax.axis_size("layer")
+    share = pixels // count
     bias_wide = jnp.broadcast_to(conv_bias[:, :, None], conv_bias.shape + (LANES,))
-    ends = relax_block(start[0], conv_weight, bias_wide)[None]
-    received, matrix_in = from_behind((ends, coarse_matrix[0]), "layer", 1)
-    leading_block = lax.axis_index("layer") == 0
-    mismatch_vector = jnp.where(leading_block, network_input - start, received - start)
-
-    def sweep_turn(counter, carried):
-        previous = from_behind(carried, "layer", 1)
-        return apply_matrix(matrix_in, previous) + mismatch_vector
-
-    correction = lax.fori_loop(0, lax.axis_size("layer") - 1, sweep_turn, mismatch_vector)
-    corrected = start + correction
-    block_final_states = relax_block(corrected[0], conv_weight, bias_wide)[None]
-    return (block_final_states[None], corrected[None])
+    state = jax.ShapeDtypeStruct((ch, pixels), jnp.float32)
+    transposed = pltpu.VMEM((pixels, ch), jnp.float32)
+    gathered = pltpu.VMEM((count, share, ch), jnp.float32)
+    final, corrected = pl.pallas_call(
+        functools.partial(cycle_kernel, count),
+        out_shape=(state, state),
+        in_specs=[pl.BlockSpec(memory_space=pltpu.VMEM)] * 5,
+        out_specs=(pl.BlockSpec(memory_space=pltpu.VMEM),) * 2,
+        scratch_shapes=[
+            pltpu.VMEM((8, ch, LANES), jnp.float32),
+            pltpu.VMEM((8, ch, LANES), jnp.float32),
+            pltpu.VMEM((ch, ch), jnp.float32),
+            transposed,
+            transposed,
+            transposed,
+            pltpu.VMEM((count, ch, ch), jnp.float32),
+            gathered,
+            gathered,
+            gathered,
+            gathered,
+            pltpu.SemaphoreType.DMA((4,)),
+            pltpu.SemaphoreType.DMA((4,)),
+        ],
+        compiler_params=pltpu.CompilerParams(
+            collective_id=0, has_side_effects=True, vmem_limit_bytes=60 << 20
+        ),
+    )(cpoints[0, 0], network_input[0], conv_weight, bias_wide, coarse_matrix[0])
+    return (final[None, None], corrected[None, None])
 
 
 def solution(mesh):

time: 706 us -> 128 us (0.18)
  waiting for transfers between devices: 502 us -> 0 us
  starting transfers between devices: 127 us -> 0 us
  Pallas kernels: 45 us -> 121 us
  matrix products: 23 us -> 0 us
    ppermute x65 -> x0, waiting for transfers between devices: 502 us -> none  [from_behind(): lax.ppermute(value, axis, [(source, source + steps) for source in range(i...]
    ppermute x65 -> x0, starting transfers between devices: 127 us -> none  [from_behind(): lax.ppermute(value, axis, [(source, source + steps) for source in range(i...]
    pallas_call x2 -> x1, Pallas kernels: 45 us -> 121 us  [on_device(): pl.pallas_call(functools.partial(cycle_kernel, count), out_shape=(state,...]
    dot_general x63 -> x0, matrix products: 23 us -> none  [apply_matrix(): jnp.einsum('cd,idp->icp', matrix, field, precision=lax.Precision.HIGHEST)]
  transfers between devices with their start and end apart: 65 -> 0, of which waited for: 65 -> 0; matrix products, arithmetic and copies ran while one was open for 0% -> 0% of each run, Pallas kernels for 0% -> 0%
where the time goes in v2:
time: 128 us; the launch traced here: 127 us
  Pallas kernels  121 us (95%)
  local copies, waits for them, and re-layouts  5.71 us (4%)
    pallas_call x1, Pallas kernels, on_device(): pl.pallas_call(functools.partial(cycle_kernel, count), out_shape=(state,...  121 us
    unnamed x2, local copies, waits for them, and re-layouts  3.34 us

profile of v2, /device:TPU:14, one launch (start us, length us, event | category | flops | bytes accessed | tf_op | source)
XLA Modules:
  0.0 126.9 jit_solution(2696735968362728676)
XLA Ops:
  0.6 2.4 %broadcast_in_dim.12.bias_ref = f32[48,64,128]{2,1,0:T(8,128)} broadcast(f32[48,64]{1,0:T(8,128)} %param.8), dimensions={0,1} | broadcast | bytes 1585152 | tf_op jit(solution)/shard_map/broadcast_in_dim | solution.py:219
  3.0 120.5 %shard_map.68 = (f32[64,1024]{1,0:T(8,128)}, f32[64,1024]{1,0:T(8,128)}) custom-call(f32[64,1024]{1,0:T(8,128)} %bitcast.5, f32[64,1024]{1,0:T(8,128)} %bitcast.6, bf16[48,64,576]{2,1,0:T(8,128)(2,1)} %weight_ref.1, f32[48,64,128]{2,1,0:T(8,128)} %broadcast_in_dim.12.bias_ref, f32[64,64]{1,0:T(8,128)} %bitcast.9), custom_call_target="tpu_custom_call" | custom-call | tf_op jit(solution)/shard_map/pallas_call | solution.py:223
  123.5 1.7 %copy.9 = f32[1,1,64,1024]{3,2,1,0:T(8,128)} copy(f32[1,1,64,1024]{3,2,1,0:T(8,128)} %bitcast.8) | data formatting | bytes 524288
  125.2 1.7 %copy.10 = f32[1,1,64,1024]{3,2,1,0:T(8,128)} copy(f32[1,1,64,1024]{3,2,1,0:T(8,128)} %bitcast.7) | data formatting | bytes 524288

commit v3 on v2

--- a/solution.py
+++ b/solution.py
@@ -90,30 +90,43 @@
     count,
     start_ref,
     input_ref,
-    weight_ref,
+    weight_hbm,
     bias_ref,
     matrix_ref,
     final_ref,
     corrected_ref,
+    weights,
+    biases,
     state,
     origin,
-    matrix_t,
-    start_t,
-    ends_t,
-    input_t,
+    starts_out,
+    ends_out,
+    input_out,
     matrices,
+    coarse_high,
+    coarse_low,
     starts,
     ends,
     chain,
     returned,
+    load_sems,
     send_sems,
     recv_sems,
 ):
     me = lax.axis_index("layer")
+    core = lax.rem(me, 2)
+    chips = count // 2
     ch, pixels = start_ref.shape
-    layers = weight_ref.shape[0]
-    share = pixels // count
-    early = layers // 4
+    layers = weights.shape[0]
+    share = pixels // 2 // count
+    early, late = layers // 6, 2 * layers // 3
+
+    loads = [
+        pltpu.make_async_copy(weight_hbm.at[part], weights.at[part], load_sems.at[number])
+        for number, part in enumerate((pl.ds(0, early), pl.ds(early, layers - early)))
+    ]
+    for load in loads:
+        load.start()
 
     def slice_of(owner):
         return pl.ds(pl.multiple_of(owner * share, share), share)
@@ -128,16 +141,18 @@
             device_id_type=pl.DeviceIdType.MESH,
         )
 
-    def peers(action):
+    def peers(action, stride=1):
         def turn(offset, unused):
-            action(lax.rem(me + offset, count))
+            action(lax.rem(me + offset * stride, count))
             return unused
 
-        lax.fori_loop(1, count, turn, 0)
+        lax.fori_loop(1, count // stride, turn, 0)
 
     def all_of(buffer, number):
-        part = buffer.at[pl.ds(0, count - 1)]
-        return push(part, part, number, lax.rem(me + 1, count))
+        return push(buffer, buffer, number, lax.rem(me + 1, count))
+
+    def packed(bands):
+        return [jnp.concatenate([bands[k], bands[k + 4]], axis=0).T for k in range(4)]
 
     barrier = pltpu.get_barrier_semaphore()
     peers(
@@ -145,33 +160,62 @@
             barrier, inc=1, device_id={"layer": peer}, device_id_type=pl.DeviceIdType.MESH
         )
     )
-    matrix_t[...] = matrix_ref[...].T
-    matrices[me] = matrix_ref[...].T
-    for band, value in enumerate(to_bands(split_lanes(start_ref[...]))):
-        state[band] = value
-        origin[band] = value
-        start_t[LANES * band : LANES * (band + 1), :] = value.T
-    for band, value in enumerate(to_bands(split_lanes(input_ref[...]))):
-        input_t[LANES * band : LANES * (band + 1), :] = value.T
-    starts[me] = start_t[slice_of(me), :]
-    conv_layers(state, weight_ref, bias_ref, 0, early)
+    turned = matrix_ref[...].T
+    matrices[core, me // 2] = jnp.concatenate([turned[: ch // 2], turned[ch // 2 :]], axis=1)
+    columns = bias_ref[...].T
+    for index in range(layers):
+        biases[index] = jnp.broadcast_to(columns[:, index : index + 1], (ch, LANES))
+    bands = to_bands(split_lanes(start_ref[...]))
+    for band in range(8):
+        state[band] = bands[band]
+        origin[band] = bands[band]
+    for part, value in enumerate(packed(bands)):
+        starts_out[LANES * part : LANES * (part + 1), :] = value
+    for part, value in enumerate(packed(to_bands(split_lanes(input_ref[...])))):
+        input_out[LANES * part : LANES * (part + 1), :] = value
+    starts[me] = starts_out[slice_of(me), :]
+    loads[0].wait()
+    conv_layers(state, weights, biases, 0, early)
 
     pl.semaphore_wait(barrier, count - 1)
-
-    def send_early(peer):
-        push(matrix_t, matrices.at[me], 0, peer).start()
-        push(start_t.at[slice_of(peer)], starts.at[me], 1, peer).start()
-
-    peers(send_early)
-    conv_layers(state, weight_ref, bias_ref, early, layers)
-
-    for band in range(8):
-        ends_t[LANES * band : LANES * (band + 1), :] = state[band].T
-    ends[me] = ends_t[slice_of(me), :]
-    peers(lambda peer: push(ends_t.at[slice_of(peer)], ends.at[me], 2, peer).start())
-    all_of(matrices, 0).wait_recv()
-    all_of(starts, 1).wait_recv()
-    all_of(ends, 2).wait_recv()
+    own = matrices.at[core, me // 2]
+    peers(lambda peer: push(own, own, 0, peer).start(), 2)
+    peers(lambda peer: push(starts_out.at[slice_of(peer)], starts.at[me], 1, peer).start())
+    loads[1].wait()
+    conv_layers(state, weights, biases, early, late)
+
+    all_of(matrices.at[0, pl.ds(0, chips - 1)], 0).wait_recv()
+    across = push(matrices.at[core], matrices.at[core], 4, me + 1 - 2 * core)
+    across.start()
+    conv_layers(state, weights, biases, late, layers)
+
+    for part, value in enumerate(packed([state[band] for band in range(8)])):
+        ends_out[LANES * part : LANES * (part + 1), :] = value
+    ends[me] = ends_out[slice_of(me), :]
+    peers(lambda peer: push(ends_out.at[slice_of(peer)], ends.at[me], 2, peer).start())
+    across.wait_recv()
+    lower = lax.broadcasted_iota(jnp.int32, (ch // 2, LANES), 1) < ch
+
+    def widen(index, unused):
+        pair = matrices[lax.rem(index, 2), index // 2]
+        swapped = pltpu.roll(pair, ch, 1)
+        wide = jnp.concatenate(
+            [
+                jnp.where(lower, pair, 0.0),
+                jnp.where(lower, swapped, 0.0),
+                jnp.where(lower, 0.0, swapped),
+                jnp.where(lower, 0.0, pair),
+            ],
+            axis=0,
+        )
+        high, low = split_float(wide)
+        coarse_high[index] = high
+        coarse_low[index] = low
+        return unused
+
+    lax.fori_loop(0, count - 1, widen, 0)
+    all_of(starts.at[pl.ds(0, count - 1)], 1).wait_recv()
+    all_of(ends.at[pl.ds(0, count - 1)], 2).wait_recv()
 
     def give(index):
         @pl.when(index != me)
@@ -179,7 +223,7 @@
             push(chain.at[index], returned.at[me], 3, index).start()
 
     def chain_step(index, current):
-        matrix_high, matrix_low = split_float(matrices[index - 1])
+        matrix_high, matrix_low = coarse_high[index - 1], coarse_low[index - 1]
         high, low = split_float(current)
         both = jnp.dot(
             jnp.concatenate([high, low], axis=0), matrix_high, preferred_element_type=jnp.float32
@@ -190,60 +234,71 @@
         give(index - 1)
         return current
 
-    first = input_t[slice_of(me), :] - starts[0]
+    first = input_out[slice_of(me), :] - starts[0]
     chain[0] = first
     lax.fori_loop(1, count, chain_step, first, unroll=3)
     give(count - 1)
     returned[me] = chain[me]
-    all_of(returned, 3).wait_recv()
-
-    corrected = []
-    gathered = returned[...].reshape(pixels, ch)
+    all_of(returned.at[pl.ds(0, count - 1)], 3).wait_recv()
+
+    gathered = returned[...].reshape(pixels // 2, LANES)
+    corrected = [None] * 8
+    for part in range(4):
+        both = gathered[LANES * part : LANES * (part + 1)].T
+        corrected[part] = origin[part] + both[:ch]
+        corrected[part + 4] = origin[part + 4] + both[ch:]
     for band in range(8):
-        part = gathered[LANES * band : LANES * (band + 1)]
-        corrected.append(origin[band] + part.T)
         state[band] = corrected[band]
     for tile, value in enumerate(from_bands(corrected)):
         corrected_ref[:, LANES * tile : LANES * (tile + 1)] = value
-    conv_layers(state, weight_ref, bias_ref, 0, layers)
+    conv_layers(state, weights, biases, 0, layers)
     for tile, value in enumerate(from_bands([state[band] for band in range(8)])):
         final_ref[:, LANES * tile : LANES * (tile + 1)] = value
-    for number, buffer in enumerate((matrices, starts, ends, returned)):
-        all_of(buffer, number).wait_send()
+    all_of(matrices.at[0, pl.ds(0, chips - 1)], 0).wait_send()
+    across.wait_send()
+    for number, buffer in ((1, starts), (2, ends), (3, returned)):
+        all_of(buffer.at[pl.ds(0, count - 1)], number).wait_send()
 
 
 def on_device(cpoints, network_input, conv_weight, conv_bias, coarse_matrix):
     ch, pixels = network_input.shape[1:]
+    layers = conv_bias.shape[0]
     count = lax.axis_size("layer")
-    share = pixels // count
-    bias_wide = jnp.broadcast_to(conv_bias[:, :, None], conv_bias.shape + (LANES,))
+    share = pixels // 2 // count
     state = jax.ShapeDtypeStruct((ch, pixels), jnp.float32)
-    transposed = pltpu.VMEM((pixels, ch), jnp.float32)
-    gathered = pltpu.VMEM((count, share, ch), jnp.float32)
+    banded = pltpu.VMEM((8, ch, LANES), jnp.float32)
+    sent = pltpu.VMEM((pixels // 2, LANES), jnp.float32)
+    gathered = pltpu.VMEM((count, share, LANES), jnp.float32)
+    wide = pltpu.VMEM((count, LANES, LANES), jnp.bfloat16)
+    vmem = pl.BlockSpec(memory_space=pltpu.VMEM)
     final, corrected = pl.pallas_call(
         functools.partial(cycle_kernel, count),
         out_shape=(state, state),
-        in_specs=[pl.BlockSpec(memory_space=pltpu.VMEM)] * 5,
-        out_specs=(pl.BlockSpec(memory_space=pltpu.VMEM),) * 2,
+        in_specs=[vmem, vmem, pl.BlockSpec(memory_space=pl.ANY), vmem, vmem],
+        out_specs=(vmem, vmem),
         scratch_shapes=[
-            pltpu.VMEM((8, ch, LANES), jnp.float32),
-            pltpu.VMEM((8, ch, LANES), jnp.float32),
-            pltpu.VMEM((ch, ch), jnp.float32),
-            transposed,
-            transposed,
-            transposed,
-            pltpu.VMEM((count, ch, ch), jnp.float32),
+            pltpu.VMEM(conv_weight.shape, conv_weight.dtype),
+            pltpu.VMEM((layers, ch, LANES), jnp.float32),
+            banded,
+            banded,
+            sent,
+            sent,
+            sent,
+            pltpu.VMEM((2, count // 2, ch // 2, LANES), jnp.float32),
+            wide,
+            wide,
             gathered,
             gathered,
             gathered,
             gathered,
-            pltpu.SemaphoreType.DMA((4,)),
-            pltpu.SemaphoreType.DMA((4,)),
+            pltpu.SemaphoreType.DMA((2,)),
+            pltpu.SemaphoreType.DMA((5,)),
+            pltpu.SemaphoreType.DMA((5,)),
         ],
         compiler_params=pltpu.CompilerParams(
             collective_id=0, has_side_effects=True, vmem_limit_bytes=60 << 20
         ),
-    )(cpoints[0, 0], network_input[0], conv_weight, bias_wide, coarse_matrix[0])
+    )(cpoints[0, 0], network_input[0], conv_weight, conv_bias, coarse_matrix[0])
     return (final[None, None], corrected[None, None])
 
 

time: 128 us -> 77.2 us (0.60)
  Pallas kernels: 121 us -> 72.8 us
  local copies, waits for them, and re-layouts: 5.71 us -> 3.34 us
    pallas_call x1, Pallas kernels: 121 us -> 72.8 us  [on_device(): pl.pallas_call(functools.partial(cycle_kernel, count), out_shape=(state,...]
    broadcast_in_dim x1 -> x0, local copies, waits for them, and re-layouts: 2.37 us -> none  [on_device(): jnp.broadcast_to(conv_bias[:, :, None], conv_bias.shape + (LANES,))]
where the time goes in v3:
time: 77.2 us; the launch traced here: 76.8 us
  Pallas kernels  72.8 us (94%)
  local copies, waits for them, and re-layouts  3.34 us (4%)
    pallas_call x1, Pallas kernels, on_device(): pl.pallas_call(functools.partial(cycle_kernel, count), out_shape=(state,...  72.8 us
    unnamed x2, local copies, waits for them, and re-layouts  3.34 us

profile of v3, /device:TPU:14, one launch (start us, length us, event | category | flops | bytes accessed | tf_op | source)
XLA Modules:
  0.0 76.8 jit_solution(4652931488109109678)
XLA Ops:
  0.6 72.8 %shard_map.68 = (f32[64,1024]{1,0:T(8,128)}, f32[64,1024]{1,0:T(8,128)}) custom-call(f32[64,1024]{1,0:T(8,128)} %bitcast.5, f32[64,1024]{1,0:T(8,128)} %bitcast.6, bf16[48,64,576]{2,1,0:T(8,128)(2,1)} %weight_hbm.1, f32[48,64]{1,0:T(8,128)} %bias_ref.1, f32[64,64]{1,0:T(8,128)} %bitcast.9), custom_call_target="tpu_custom_call" | custom-call | tf_op jit(solution)/shard_map/pallas_call | solution.py:274
  73.4 1.7 %copy.9 = f32[1,1,64,1024]{3,2,1,0:T(8,128)} copy(f32[1,1,64,1024]{3,2,1,0:T(8,128)} %bitcast.8) | data formatting | bytes 524288
  75.1 1.7 %copy.10 = f32[1,1,64,1024]{3,2,1,0:T(8,128)} copy(f32[1,1,64,1024]{3,2,1,0:T(8,128)} %bitcast.7) | data formatting | bytes 524288

commit v4 on v3

--- a/solution.py
+++ b/solution.py
@@ -43,7 +43,7 @@
     return [value[:, LANES * k : LANES * (k + 1)] for k in range(value.shape[1] // LANES)]
 
 
-def conv_layers(state_ref, weight_ref, bias_ref, first, last, unroll=1):
+def conv_layers(state_ref, weight_ref, bias_ref, first, last, unroll):
     ch = state_ref.shape[1]
     lane = lax.broadcasted_iota(jnp.int32, (ch, LANES), 1)
     column = lane % SIDE
@@ -57,9 +57,11 @@
         left, mid, right = [], [], []
         for band in range(8):
             value = state_ref[band]
-            left.append(jnp.where(not_first, pltpu.roll(value, 1, 1), 0.0).astype(jnp.bfloat16))
-            mid.append(value.astype(jnp.bfloat16))
-            right.append(jnp.where(not_last, pltpu.roll(value, LANES - 1, 1), 0.0).astype(jnp.bfloat16))
+            value = value.astype(jnp.bfloat16)
+            zero = jnp.zeros_like(value)
+            left.append(jnp.where(not_first, pltpu.roll(value, 1, 1), zero))
+            mid.append(value)
+            right.append(jnp.where(not_last, pltpu.roll(value, LANES - 1, 1), zero))
         taps = []
         for pair in range(4):
             stack = jnp.concatenate(
@@ -120,6 +122,7 @@
     layers = weights.shape[0]
     share = pixels // 2 // count
     early, late = layers // 6, 2 * layers // 3
+    unroll = 4 if early % 4 == 0 else 1
 
     loads = [
         pltpu.make_async_copy(weight_hbm.at[part], weights.at[part], load_sems.at[number])
@@ -146,7 +149,7 @@
             action(lax.rem(me + offset * stride, count))
             return unused
 
-        lax.fori_loop(1, count // stride, turn, 0)
+        lax.fori_loop(1, count // stride, turn, 0, unroll=3 if stride == 1 else 1)
 
     def all_of(buffer, number):
         return push(buffer, buffer, number, lax.rem(me + 1, count))
@@ -171,28 +174,28 @@
         origin[band] = bands[band]
     for part, value in enumerate(packed(bands)):
         starts_out[LANES * part : LANES * (part + 1), :] = value
-    for part, value in enumerate(packed(to_bands(split_lanes(input_ref[...])))):
-        input_out[LANES * part : LANES * (part + 1), :] = value
     starts[me] = starts_out[slice_of(me), :]
     loads[0].wait()
-    conv_layers(state, weights, biases, 0, early)
+    conv_layers(state, weights, biases, 0, early, unroll)
 
     pl.semaphore_wait(barrier, count - 1)
     own = matrices.at[core, me // 2]
     peers(lambda peer: push(own, own, 0, peer).start(), 2)
     peers(lambda peer: push(starts_out.at[slice_of(peer)], starts.at[me], 1, peer).start())
     loads[1].wait()
-    conv_layers(state, weights, biases, early, late)
+    conv_layers(state, weights, biases, early, late, unroll)
 
     all_of(matrices.at[0, pl.ds(0, chips - 1)], 0).wait_recv()
     across = push(matrices.at[core], matrices.at[core], 4, me + 1 - 2 * core)
     across.start()
-    conv_layers(state, weights, biases, late, layers)
+    conv_layers(state, weights, biases, late, layers, unroll)
 
     for part, value in enumerate(packed([state[band] for band in range(8)])):
         ends_out[LANES * part : LANES * (part + 1), :] = value
     ends[me] = ends_out[slice_of(me), :]
     peers(lambda peer: push(ends_out.at[slice_of(peer)], ends.at[me], 2, peer).start())
+    for part, value in enumerate(packed(to_bands(split_lanes(input_ref[...])))):
+        input_out[LANES * part : LANES * (part + 1), :] = value
     across.wait_recv()
     lower = lax.broadcasted_iota(jnp.int32, (ch // 2, LANES), 1) < ch
 
@@ -213,7 +216,7 @@
         coarse_low[index] = low
         return unused
 
-    lax.fori_loop(0, count - 1, widen, 0)
+    lax.fori_loop(0, count - 1, widen, 0, unroll=3)
     all_of(starts.at[pl.ds(0, count - 1)], 1).wait_recv()
     all_of(ends.at[pl.ds(0, count - 1)], 2).wait_recv()
 
@@ -251,7 +254,7 @@
         state[band] = corrected[band]
     for tile, value in enumerate(from_bands(corrected)):
         corrected_ref[:, LANES * tile : LANES * (tile + 1)] = value
-    conv_layers(state, weights, biases, 0, layers)
+    conv_layers(state, weights, biases, 0, layers, unroll)
     for tile, value in enumerate(from_bands([state[band] for band in range(8)])):
         final_ref[:, LANES * tile : LANES * (tile + 1)] = value
     all_of(matrices.at[0, pl.ds(0, chips - 1)], 0).wait_send()

time: 77.2 us -> 76.2 us (0.987)
  Pallas kernels: 72.8 us -> 71.8 us
    pallas_call x1, Pallas kernels: 72.8 us -> 71.8 us  [on_device(): pl.pallas_call(functools.partial(cycle_kernel, count), out_shape=(state,...]
where the time goes in v4:
time: 76.2 us; the launch traced here: 75.8 us
  Pallas kernels  71.8 us (94%)
  local copies, waits for them, and re-layouts  3.34 us (4%)
    pallas_call x1, Pallas kernels, on_device(): pl.pallas_call(functools.partial(cycle_kernel, count), out_shape=(state,...  71.8 us
    unnamed x2, local copies, waits for them, and re-layouts  3.34 us

profile of v4, /device:TPU:14, one launch (start us, length us, event | category | flops | bytes accessed | tf_op | source)
XLA Modules:
  0.0 75.8 jit_solution(5137852698194406217)
XLA Ops:
  0.6 71.8 %shard_map.68 = (f32[64,1024]{1,0:T(8,128)}, f32[64,1024]{1,0:T(8,128)}) custom-call(f32[64,1024]{1,0:T(8,128)} %bitcast.5, f32[64,1024]{1,0:T(8,128)} %bitcast.6, bf16[48,64,576]{2,1,0:T(8,128)(2,1)} %weight_hbm.1, f32[48,64]{1,0:T(8,128)} %bias_ref.1, f32[64,64]{1,0:T(8,128)} %bitcast.9), custom_call_target="tpu_custom_call" | custom-call | tf_op jit(solution)/shard_map/pallas_call | solution.py:277
  72.5 1.7 %copy.9 = f32[1,1,64,1024]{3,2,1,0:T(8,128)} copy(f32[1,1,64,1024]{3,2,1,0:T(8,128)} %bitcast.8) | data formatting | bytes 524288
  74.1 1.7 %copy.10 = f32[1,1,64,1024]{3,2,1,0:T(8,128)} copy(f32[1,1,64,1024]{3,2,1,0:T(8,128)} %bitcast.7) | data formatting | bytes 524288

commit v5 on v4

--- a/solution.py
+++ b/solution.py
@@ -95,8 +95,8 @@
     weight_hbm,
     bias_ref,
     matrix_ref,
-    final_ref,
-    corrected_ref,
+    change_ref,
+    correction_ref,
     weights,
     biases,
     state,
@@ -245,18 +245,19 @@
     all_of(returned.at[pl.ds(0, count - 1)], 3).wait_recv()
 
     gathered = returned[...].reshape(pixels // 2, LANES)
-    corrected = [None] * 8
+    correction = [None] * 8
     for part in range(4):
         both = gathered[LANES * part : LANES * (part + 1)].T
-        corrected[part] = origin[part] + both[:ch]
-        corrected[part + 4] = origin[part + 4] + both[ch:]
+        correction[part] = both[:ch]
+        correction[part + 4] = both[ch:]
     for band in range(8):
-        state[band] = corrected[band]
-    for tile, value in enumerate(from_bands(corrected)):
-        corrected_ref[:, LANES * tile : LANES * (tile + 1)] = value
+        state[band] = origin[band] + correction[band]
+        origin[band] = state[band]
+    for tile, value in enumerate(from_bands(correction)):
+        correction_ref[:, LANES * tile : LANES * (tile + 1)] = value
     conv_layers(state, weights, biases, 0, layers, unroll)
-    for tile, value in enumerate(from_bands([state[band] for band in range(8)])):
-        final_ref[:, LANES * tile : LANES * (tile + 1)] = value
+    for tile, value in enumerate(from_bands([state[band] - origin[band] for band in range(8)])):
+        change_ref[:, LANES * tile : LANES * (tile + 1)] = value
     all_of(matrices.at[0, pl.ds(0, chips - 1)], 0).wait_send()
     across.wait_send()
     for number, buffer in ((1, starts), (2, ends), (3, returned)):
@@ -274,7 +275,7 @@
     gathered = pltpu.VMEM((count, share, LANES), jnp.float32)
     wide = pltpu.VMEM((count, LANES, LANES), jnp.bfloat16)
     vmem = pl.BlockSpec(memory_space=pltpu.VMEM)
-    final, corrected = pl.pallas_call(
+    change, correction = pl.pallas_call(
         functools.partial(cycle_kernel, count),
         out_shape=(state, state),
         in_specs=[vmem, vmem, pl.BlockSpec(memory_space=pl.ANY), vmem, vmem],
@@ -302,7 +303,8 @@
             collective_id=0, has_side_effects=True, vmem_limit_bytes=60 << 20
         ),
     )(cpoints[0, 0], network_input[0], conv_weight, conv_bias, coarse_matrix[0])
-    return (final[None, None], corrected[None, None])
+    corrected = cpoints[0, 0] + correction
+    return ((corrected + change)[None, None], corrected[None, None])
 
 
 def solution(mesh):

time: 76.2 us -> 74.8 us (0.982)
  local copies, waits for them, and re-layouts: 3.34 us -> 0.01 us
  other arithmetic: 0 us -> 1.88 us
    unnamed x2, local copies, waits for them, and re-layouts: 3.34 us -> 0.01 us
    broadcast_in_dim x0 -> x1, other arithmetic: none -> 1.88 us  [on_device(): return ((corrected + change)[None, None], corrected[None, None])]
where the time goes in v5:
time: 74.8 us; the launch traced here: 74.4 us
  Pallas kernels  71.8 us (96%)
  other arithmetic  1.88 us (3%)
    pallas_call x1, Pallas kernels, on_device(): pl.pallas_call(functools.partial(cycle_kernel, count), out_shape=(state,...  71.8 us
    broadcast_in_dim x1, other arithmetic, on_device(): return ((corrected + change)[None, None], corrected[None, None])  1.88 us

profile of v5, /device:TPU:14, one launch (start us, length us, event | category | flops | bytes accessed | tf_op | source)
XLA Modules:
  0.0 74.4 jit_solution(14246995751658315387)
XLA Ops:
  0.6 0.0 copy-start
  0.6 71.8 %shard_map.68 = (f32[64,1024]{1,0:T(8,128)}, f32[64,1024]{1,0:T(8,128)}) custom-call(f32[64,1024]{1,0:T(8,128)} %bitcast.9, f32[64,1024]{1,0:T(8,128)} %bitcast.10, bf16[48,64,576]{2,1,0:T(8,128)(2,1)} %weight_hbm.1, f32[48,64]{1,0:T(8,128)} %bias_ref.1, f32[64,64]{1,0:T(8,128)} %bitcast.11), custom_call_target="tpu_custom_call" | custom-call | tf_op jit(solution)/shard_map/pallas_call | solution.py:278
  72.5 0.0 copy-done
  72.5 1.9 %add_bitcast_fusion.1 = (f32[1,1,64,1024]{3,2,1,0:T(8,128)}, f32[1,1,64,1024]{3,2,1,0:T(8,128)}) fusion(f32[64,1024]{1,0:T(8,128)} %get-tuple-element.4, f32[1,1,64,1024]{3,2,1,0:T(8,128)S(1)} %copy-done, f32[64,1024]{1,0:T(8,128)} %get-tuple-element.5), kind=kLoop, calls=%fused_computation.1 | loop fusion | flops 131072 | bytes 1310720 | tf_op jit(solution)/shard_map/broadcast_in_dim | solution.py:307
Async XLA Ops:
  0.6 71.9 %copy-start = (f32[1,1,64,1024]{3,2,1,0:T(8,128)S(1)}, f32[1,1,64,1024]{3,2,1,0:T(8,128)}, u32[]{:S(2)}) copy-start(f32[1,1,64,1024]{3,2,1,0:T(8,128)} %param.5) | copy-start | bytes 786436

commit v6 on v5

--- a/solution.py
+++ b/solution.py
@@ -43,7 +43,7 @@
     return [value[:, LANES * k : LANES * (k + 1)] for k in range(value.shape[1] // LANES)]
 
 
-def conv_layers(state_ref, weight_ref, bias_ref, first, last, unroll):
+def conv_layers(state_ref, weight_ref, rows_ref, bias_ref, first, last, unroll, fresh):
     ch = state_ref.shape[1]
     lane = lax.broadcasted_iota(jnp.int32, (ch, LANES), 1)
     column = lane % SIDE
@@ -51,8 +51,12 @@
     below, above = lane >= SIDE, lane < LANES - SIDE
 
     def layer(index, unused):
-        weight = weight_ref[index]
-        rows = jnp.concatenate([weight[:, 3 * ch * k : 3 * ch * (k + 1)] for k in range(3)], axis=0)
+        if fresh:
+            weight = weight_ref[index]
+            rows = jnp.concatenate([weight[:, 3 * ch * k : 3 * ch * (k + 1)] for k in range(3)], axis=0)
+            rows_ref[index] = rows
+        else:
+            rows = rows_ref[index]
         bias = bias_ref[index]
         left, mid, right = [], [], []
         for band in range(8):
@@ -98,6 +102,7 @@
     change_ref,
     correction_ref,
     weights,
+    stacked,
     biases,
     state,
     origin,
@@ -121,7 +126,7 @@
     ch, pixels = start_ref.shape
     layers = weights.shape[0]
     share = pixels // 2 // count
-    early, late = layers // 6, 2 * layers // 3
+    early, late = layers // 6, 5 * layers // 6
     unroll = 4 if early % 4 == 0 else 1
 
     loads = [
@@ -176,19 +181,19 @@
         starts_out[LANES * part : LANES * (part + 1), :] = value
     starts[me] = starts_out[slice_of(me), :]
     loads[0].wait()
-    conv_layers(state, weights, biases, 0, early, unroll)
+    conv_layers(state, weights, stacked, biases, 0, early, unroll, True)
 
     pl.semaphore_wait(barrier, count - 1)
     own = matrices.at[core, me // 2]
     peers(lambda peer: push(own, own, 0, peer).start(), 2)
     peers(lambda peer: push(starts_out.at[slice_of(peer)], starts.at[me], 1, peer).start())
     loads[1].wait()
-    conv_layers(state, weights, biases, early, late, unroll)
+    conv_layers(state, weights, stacked, biases, early, late, unroll, True)
 
     all_of(matrices.at[0, pl.ds(0, chips - 1)], 0).wait_recv()
     across = push(matrices.at[core], matrices.at[core], 4, me + 1 - 2 * core)
     across.start()
-    conv_layers(state, weights, biases, late, layers, unroll)
+    conv_layers(state, weights, stacked, biases, late, layers, unroll, True)
 
     for part, value in enumerate(packed([state[band] for band in range(8)])):
         ends_out[LANES * part : LANES * (part + 1), :] = value
@@ -255,7 +260,7 @@
         origin[band] = state[band]
     for tile, value in enumerate(from_bands(correction)):
         correction_ref[:, LANES * tile : LANES * (tile + 1)] = value
-    conv_layers(state, weights, biases, 0, layers, unroll)
+    conv_layers(state, weights, stacked, biases, 0, layers, unroll, False)
     for tile, value in enumerate(from_bands([state[band] - origin[band] for band in range(8)])):
         change_ref[:, LANES * tile : LANES * (tile + 1)] = value
     all_of(matrices.at[0, pl.ds(0, chips - 1)], 0).wait_send()
@@ -282,6 +287,7 @@
         out_specs=(vmem, vmem),
         scratch_shapes=[
             pltpu.VMEM(conv_weight.shape, conv_weight.dtype),
+            pltpu.VMEM((layers, 3 * ch, 3 * ch), conv_weight.dtype),
             pltpu.VMEM((layers, ch, LANES), jnp.float32),
             banded,
             banded,

time: 74.8 us -> 71.4 us (0.955)
  Pallas kernels: 71.8 us -> 68.4 us
    pallas_call x1, Pallas kernels: 71.8 us -> 68.4 us  [on_device(): pl.pallas_call(functools.partial(cycle_kernel, count), out_shape=(state,...]
where the time goes in v6:
time: 71.4 us; the launch traced here: 71 us
  Pallas kernels  68.4 us (96%)
  other arithmetic  1.88 us (3%)
    pallas_call x1, Pallas kernels, on_device(): pl.pallas_call(functools.partial(cycle_kernel, count), out_shape=(state,...  68.4 us
    broadcast_in_dim x1, other arithmetic, on_device(): return ((corrected + change)[None, None], corrected[None, None])  1.88 us

profile of v6, /device:TPU:14, one launch (start us, length us, event | category | flops | bytes accessed | tf_op | source)
XLA Modules:
  0.0 71.0 jit_solution(11383505123733862499)
XLA Ops:
  0.6 0.0 copy-start
  0.6 68.4 %shard_map.68 = (f32[64,1024]{1,0:T(8,128)}, f32[64,1024]{1,0:T(8,128)}) custom-call(f32[64,1024]{1,0:T(8,128)} %bitcast.9, f32[64,1024]{1,0:T(8,128)} %bitcast.10, bf16[48,64,576]{2,1,0:T(8,128)(2,1)} %weight_hbm.1, f32[48,64]{1,0:T(8,128)} %bias_ref.1, f32[64,64]{1,0:T(8,128)} %bitcast.11), custom_call_target="tpu_custom_call" | custom-call | tf_op jit(solution)/shard_map/pallas_call | solution.py:283
  69.1 0.0 copy-done
  69.1 1.9 %add_bitcast_fusion.1 = (f32[1,1,64,1024]{3,2,1,0:T(8,128)}, f32[1,1,64,1024]{3,2,1,0:T(8,128)}) fusion(f32[64,1024]{1,0:T(8,128)} %get-tuple-element.4, f32[1,1,64,1024]{3,2,1,0:T(8,128)S(1)} %copy-done, f32[64,1024]{1,0:T(8,128)} %get-tuple-element.5), kind=kLoop, calls=%fused_computation.1 | loop fusion | flops 131072 | bytes 1310720 | tf_op jit(solution)/shard_map/broadcast_in_dim | solution.py:313
Async XLA Ops:
  0.6 68.4 %copy-start = (f32[1,1,64,1024]{3,2,1,0:T(8,128)S(1)}, f32[1,1,64,1024]{3,2,1,0:T(8,128)}, u32[]{:S(2)}) copy-start(f32[1,1,64,1024]{3,2,1,0:T(8,128)} %param.5) | copy-start | bytes 786436

commit v7 on v6

--- a/solution.py
+++ b/solution.py
@@ -122,6 +122,7 @@
 ):
     me = lax.axis_index("layer")
     core = lax.rem(me, 2)
+    crowd = min(8, count)
     chips = count // 2
     ch, pixels = start_ref.shape
     layers = weights.shape[0]
@@ -139,12 +140,12 @@
     def slice_of(owner):
         return pl.ds(pl.multiple_of(owner * share, share), share)
 
-    def push(source, target, number, peer):
+    def push(source, target, number, peer, arrival=None):
         return pltpu.make_async_remote_copy(
             src_ref=source,
             dst_ref=target,
             send_sem=send_sems.at[number],
-            recv_sem=recv_sems.at[number],
+            recv_sem=recv_sems.at[number if arrival is None else arrival],
             device_id={"layer": peer},
             device_id_type=pl.DeviceIdType.MESH,
         )
@@ -197,8 +198,9 @@
 
     for part, value in enumerate(packed([state[band] for band in range(8)])):
         ends_out[LANES * part : LANES * (part + 1), :] = value
-    ends[me] = ends_out[slice_of(me), :]
-    peers(lambda peer: push(ends_out.at[slice_of(peer)], ends.at[me], 2, peer).start())
+    arrival = 5 + me // crowd
+    peers(lambda peer: push(ends_out.at[slice_of(peer)], ends.at[me], 2, peer, arrival).start())
+    pltpu.make_async_copy(ends_out.at[slice_of(me)], ends.at[me], recv_sems.at[arrival]).start()
     for part, value in enumerate(packed(to_bands(split_lanes(input_ref[...])))):
         input_out[LANES * part : LANES * (part + 1), :] = value
     across.wait_recv()
@@ -223,7 +225,6 @@
 
     lax.fori_loop(0, count - 1, widen, 0, unroll=3)
     all_of(starts.at[pl.ds(0, count - 1)], 1).wait_recv()
-    all_of(ends.at[pl.ds(0, count - 1)], 2).wait_recv()
 
     def give(index):
         @pl.when(index != me)
@@ -244,7 +245,17 @@
 
     first = input_out[slice_of(me), :] - starts[0]
     chain[0] = first
-    lax.fori_loop(1, count, chain_step, first, unroll=3)
+
+    def crowd_steps(group, current, steps):
+        part = ends.at[pl.ds(group * crowd, crowd)]
+        push(part, part, 2, lax.rem(me + 1, count), 5 + group).wait_recv()
+        for step in range(1, steps + 1):
+            current = chain_step(group * crowd + step, current)
+        return current
+
+    groups = count // crowd
+    current = lax.fori_loop(0, groups - 1, lambda group, value: crowd_steps(group, value, crowd), first)
+    crowd_steps(groups - 1, current, crowd - 1)
     give(count - 1)
     returned[me] = chain[me]
     all_of(returned.at[pl.ds(0, count - 1)], 3).wait_recv()
@@ -303,7 +314,7 @@
             gathered,
             pltpu.SemaphoreType.DMA((2,)),
             pltpu.SemaphoreType.DMA((5,)),
-            pltpu.SemaphoreType.DMA((5,)),
+            pltpu.SemaphoreType.DMA((5 + count // min(8, count),)),
         ],
         compiler_params=pltpu.CompilerParams(
             collective_id=0, has_side_effects=True, vmem_limit_bytes=60 << 20

time: 71.4 us -> 70.2 us (0.983)
  Pallas kernels: 68.4 us -> 67.2 us
    pallas_call x1, Pallas kernels: 68.4 us -> 67.2 us  [on_device(): pl.pallas_call(functools.partial(cycle_kernel, count), out_shape=(state,...]
where the time goes in v7:
time: 70.2 us; the launch traced here: 69.7 us
  Pallas kernels  67.2 us (96%)
  other arithmetic  1.88 us (3%)
    pallas_call x1, Pallas kernels, on_device(): pl.pallas_call(functools.partial(cycle_kernel, count), out_shape=(state,...  67.2 us
    broadcast_in_dim x1, other arithmetic, on_device(): return ((corrected + change)[None, None], corrected[None, None])  1.88 us

profile of v7, /device:TPU:14, one launch (start us, length us, event | category | flops | bytes accessed | tf_op | source)
XLA Modules:
  0.0 69.7 jit_solution(12019712871918856052)
XLA Ops:
  0.6 0.0 copy-start
  0.6 67.2 %shard_map.68 = (f32[64,1024]{1,0:T(8,128)}, f32[64,1024]{1,0:T(8,128)}) custom-call(f32[64,1024]{1,0:T(8,128)} %bitcast.9, f32[64,1024]{1,0:T(8,128)} %bitcast.10, bf16[48,64,576]{2,1,0:T(8,128)(2,1)} %weight_hbm.1, f32[48,64]{1,0:T(8,128)} %bias_ref.1, f32[64,64]{1,0:T(8,128)} %bitcast.11), custom_call_target="tpu_custom_call" | custom-call | tf_op jit(solution)/shard_map/pallas_call | solution.py:294
  67.9 0.0 copy-done
  67.9 1.9 %add_bitcast_fusion.1 = (f32[1,1,64,1024]{3,2,1,0:T(8,128)}, f32[1,1,64,1024]{3,2,1,0:T(8,128)}) fusion(f32[64,1024]{1,0:T(8,128)} %get-tuple-element.4, f32[1,1,64,1024]{3,2,1,0:T(8,128)S(1)} %copy-done, f32[64,1024]{1,0:T(8,128)} %get-tuple-element.5), kind=kLoop, calls=%fused_computation.1 | loop fusion | flops 131072 | bytes 1310720 | tf_op jit(solution)/shard_map/broadcast_in_dim | solution.py:324
Async XLA Ops:
  0.6 67.2 %copy-start = (f32[1,1,64,1024]{3,2,1,0:T(8,128)S(1)}, f32[1,1,64,1024]{3,2,1,0:T(8,128)}, u32[]{:S(2)}) copy-start(f32[1,1,64,1024]{3,2,1,0:T(8,128)} %param.5) | copy-start | bytes 786436

commit v8 on v7

--- a/solution.py
+++ b/solution.py
@@ -127,7 +127,7 @@
     ch, pixels = start_ref.shape
     layers = weights.shape[0]
     share = pixels // 2 // count
-    early, late = layers // 6, 5 * layers // 6
+    early, late = layers // 6, 11 * layers // 12
     unroll = 4 if early % 4 == 0 else 1
 
     loads = [

time: 70.2 us -> 70.5 us (level)
  no operation moved by 1% of the time
where the time goes in v8:
time: 70.5 us; the launch traced here: 70 us
  Pallas kernels  67.5 us (96%)
  other arithmetic  1.88 us (3%)
    pallas_call x1, Pallas kernels, on_device(): pl.pallas_call(functools.partial(cycle_kernel, count), out_shape=(state,...  67.5 us
    broadcast_in_dim x1, other arithmetic, on_device(): return ((corrected + change)[None, None], corrected[None, None])  1.88 us

profile of v8, /device:TPU:14, one launch (start us, length us, event | category | flops | bytes accessed | tf_op | source)
XLA Modules:
  0.0 70.0 jit_solution(4463790263647289240)
XLA Ops:
  0.6 0.0 copy-start
  0.6 67.5 %shard_map.68 = (f32[64,1024]{1,0:T(8,128)}, f32[64,1024]{1,0:T(8,128)}) custom-call(f32[64,1024]{1,0:T(8,128)} %bitcast.9, f32[64,1024]{1,0:T(8,128)} %bitcast.10, bf16[48,64,576]{2,1,0:T(8,128)(2,1)} %weight_hbm.1, f32[48,64]{1,0:T(8,128)} %bias_ref.1, f32[64,64]{1,0:T(8,128)} %bitcast.11), custom_call_target="tpu_custom_call" | custom-call | tf_op jit(solution)/shard_map/pallas_call | solution.py:294
  68.2 0.0 copy-done
  68.2 1.9 %add_bitcast_fusion.1 = (f32[1,1,64,1024]{3,2,1,0:T(8,128)}, f32[1,1,64,1024]{3,2,1,0:T(8,128)}) fusion(f32[64,1024]{1,0:T(8,128)} %get-tuple-element.4, f32[1,1,64,1024]{3,2,1,0:T(8,128)S(1)} %copy-done, f32[64,1024]{1,0:T(8,128)} %get-tuple-element.5), kind=kLoop, calls=%fused_computation.1 | loop fusion | flops 131072 | bytes 1310720 | tf_op jit(solution)/shard_map/broadcast_in_dim | solution.py:324
Async XLA Ops:
  0.6 67.5 %copy-start = (f32[1,1,64,1024]{3,2,1,0:T(8,128)S(1)}, f32[1,1,64,1024]{3,2,1,0:T(8,128)}, u32[]{:S(2)}) copy-start(f32[1,1,64,1024]{3,2,1,0:T(8,128)} %param.5) | copy-start | bytes 786436
